TPU v7x, 32 devices: a whole 2x2x4 slice. The times are simulated.
32 devices in a mesh: genome: 4 (over z), trow: 2 (over core), tcol: 4 (over y, x).
Axes of the slice: x: 2, y: 2, z: 4, core: 2. Of those that a mesh axis runs over, the one named last changes fastest.
Arguments:
- ldscore: float32 [4096], P('genome'), may hold values from 1 to 100
- zscores: bfloat16 [4096, 4096], P('genome', ('trow', 'tcol')), may hold values from -30 to 30
Outputs:
- rg: float32 [2, 2048, 2, 2048], P('trow', 'genome', None, 'tcol')
- rg_se: float32 [2, 2048, 2, 2048], P('trow', 'genome', None, 'tcol')
All inputs are finite; a program needn't handle non-finite values.
Results may differ from a plain program's by a relative error of at most 0.038.
Values may be sent and summed in bfloat16 or wider, within the bound.
No kernel may reach another device: no remote copies, remote signals or barrier semaphores. Data moves between devices by JAX's collectives and lax.ppermute only.
A program may use at most 192 MiB of HBM per device.

v0:
```python
import jax
import jax.numpy as jnp
from jax import lax
from jax.sharding import PartitionSpec as P

floor_value = 0.002


def contract(left, right):
    return lax.dot_general(
        left, right, (((0,), (0,)), ((), ())), preferred_element_type=jnp.float32
    )


def slope_fit(inv_sum, ld_sum, y_sum, l_sum, count):
    return (inv_sum * l_sum - count * y_sum) / (inv_sum * ld_sum - count * count)


def weights_for(herit_pos, ld_column):
    return (1.0 / (1.0 + herit_pos[None, :] * ld_column[:, None])).astype(jnp.bfloat16)


def coupling(tiles):
    return (tiles[2] * tiles[1] - tiles[3] * tiles[0]) / (tiles[2] * tiles[4] - tiles[3] * tiles[3])


def per_device(ldscore, zscores):
    blocks = lax.axis_size("genome")
    grid_rows = lax.axis_size("trow")
    grid_cols = lax.axis_size("tcol")
    snp_count = zscores.shape[0]
    shard_width = zscores.shape[1]
    traits = shard_width * grid_rows * grid_cols
    row_width = traits // grid_rows
    row_share = row_width // blocks
    row_index = lax.axis_index("trow")
    col_index = lax.axis_index("tcol")
    genome_index = lax.axis_index("genome")
    ld_weight = 1.0 / ldscore
    z_float = zscores.astype(jnp.float32)
    z_square = z_float * z_float
    own_stats = jnp.stack(
        [jnp.sum(z_square * ld_weight[:, None], axis=0), jnp.sum(z_square, axis=0)]
    )
    own_scalars = jnp.stack([jnp.sum(ld_weight), jnp.sum(ldscore)])
    all_stats, all_scalars = (
        lax.all_gather(own_stats[None], ("genome", "trow", "tcol"), axis=0, tiled=True),
        lax.all_gather(own_scalars[None], ("genome", "trow", "tcol"), axis=0, tiled=True),
    )
    all_stats = all_stats.reshape(blocks, grid_rows * grid_cols, 2, shard_width)
    all_stats = all_stats.transpose(0, 2, 1, 3).reshape(blocks, 2, traits)
    all_scalars = all_scalars.reshape(blocks, grid_rows * grid_cols, 2)[:, 0, :]
    total_stats = jnp.sum(all_stats, axis=0)
    total_scalars = jnp.sum(all_scalars, axis=0)
    herit_full = slope_fit(
        total_scalars[0],
        total_scalars[1],
        total_stats[0],
        total_stats[1],
        float(snp_count * blocks),
    )
    rest_stats = total_stats[None] - all_stats
    rest_scalars = total_scalars[None] - all_scalars
    herit_del = slope_fit(
        rest_scalars[:, 0:1],
        rest_scalars[:, 1:2],
        rest_stats[:, 0],
        rest_stats[:, 1],
        float(snp_count * (blocks - 1)),
    )
    herit_pos = jnp.maximum(herit_full, 0.0)
    col_z = lax.all_gather(zscores, "trow", axis=1, tiled=True)
    col_herit = lax.dynamic_index_in_dim(
        herit_pos.reshape(grid_rows, grid_cols, shard_width), col_index, 1, keepdims=False
    ).reshape(-1)
    col_u = weights_for(col_herit, ldscore)
    col_zu = (col_z.astype(jnp.float32) * col_u.astype(jnp.float32)).astype(jnp.bfloat16)
    piece = lax.all_gather(zscores, "tcol", axis=1, tiled=True)
    herit_rows = lax.dynamic_slice_in_dim(herit_pos, row_index * row_width, piece.shape[1])
    row_u = weights_for(herit_rows, ldscore)
    u_float = row_u.astype(jnp.float32)
    scaled = piece.astype(jnp.float32) * u_float
    row_zu = scaled.astype(jnp.bfloat16)
    row_scaled = (scaled * ld_weight[:, None]).astype(jnp.bfloat16)
    products = [contract(row_scaled, col_zu), contract(row_zu, col_zu)]
    row_inv = (u_float * ld_weight[:, None]).astype(jnp.bfloat16)
    row_ld = (u_float * ldscore[:, None]).astype(jnp.bfloat16)
    products = products + [
        contract(row_inv, col_u),
        contract(row_u, col_u),
        contract(row_ld, col_u),
    ]
    sums = jnp.stack(products)
    sums = sums.astype(jnp.bfloat16)[:, None]
    row_start = row_index * row_width + genome_index * row_share
    tiles = lax.all_to_all(sums, "genome", split_axis=2, concat_axis=1, tiled=True)
    tile_values = tiles.astype(jnp.float32)
    totals = jnp.sum(tile_values, axis=1)
    deleted = totals[:, None] - tile_values
    full_g = coupling(totals)
    del_g = coupling(deleted)
    herit_floor = jnp.maximum(herit_full, floor_value)
    del_floor = jnp.maximum(herit_del, floor_value)
    rows_full = lax.dynamic_slice_in_dim(herit_floor, row_start, row_share)
    cols_full = lax.dynamic_index_in_dim(
        herit_floor.reshape(grid_rows, grid_cols, shard_width), col_index, 1, keepdims=False
    ).reshape(-1)
    rows_del = lax.dynamic_slice_in_dim(del_floor, row_start, row_share, axis=1)
    cols_del = lax.dynamic_index_in_dim(
        del_floor.reshape(blocks, grid_rows, grid_cols, shard_width), col_index, 2, keepdims=False
    ).reshape(blocks, -1)
    rg_tile = full_g / jnp.sqrt(rows_full[:, None] * cols_full[None, :])
    rg_del = del_g / jnp.sqrt(rows_del[:, :, None] * cols_del[:, None, :])
    mean_del = jnp.mean(rg_del, axis=0)
    differ = rg_del - mean_del[None]
    spread = jnp.sum(differ * differ, axis=0)
    se_tile = jnp.sqrt((blocks - 1) / blocks * spread)
    out_shape = (1, row_share, grid_rows, shard_width)
    return (rg_tile.reshape(out_shape), se_tile.reshape(out_shape))


def solution(mesh):
    return jax.shard_map(
        per_device,
        mesh=mesh,
        in_specs=(P("genome"), P("genome", ("trow", "tcol"))),
        out_specs=(P("trow", "genome", None, "tcol"), P("trow", "genome", None, "tcol")),
        check_vma=False,
    )
```

profile of v0, /device:TPU:0, one launch (start us, length us, event | category | flops | bytes accessed | tf_op | source)
XLA Modules:
  0.0 1032.2 jit_solution(11515729871586139848)
XLA Ops:
  7.2 0.0 all-gather.8.cloned.1.call-start
  7.2 0.7 all-gather.8.cloned.1.call-update
  7.9 0.0 all-gather.6.cloned.1.call-start
  7.9 0.7 all-gather.6.cloned.1.call-update
  8.7 1.3 fusion.41
  10.0 1.5 maximum_dynamic-update-slice_fusion
  11.4 42.1 %all-reduce = f32[64]{0:T(128)S(1)} all-reduce(f32[64]{0:T(128)S(1)} %maximum_dynamic-update-slice_fusion), channel_id=2, replica_groups=mesh['genome'=4,'trow'=2,'tcol'=4] {'genome','trow','tcol'}, use_global_device_ids=true, to_apply=%add | all-reduce | flops 64 | bytes 512
  53.5 0.1 reshape.288
  53.6 0.6 fusion.49
  55.5 1.6 multiply_reduce_fusion.1
  57.2 67.2 %all-gather.2 = f32[32,2,512]{2,1,0:T(2,128)S(1)} all-gather(f32[1,2,512]{2,1,0:T(2,128)S(1)} %maximum_bitcast_fusion), channel_id=3, replica_groups=mesh['genome'=4,'trow'=2,'tcol'=4] {'genome','trow','tcol'}, dimensions={0}, use_global_device_ids=true | all-gather | bytes 135168 | tf_op jit(solution)/shard_map/all_gather | solution.py:47
  124.4 0.7 fusion.40
  125.2 0.0 all-gather.8.cloned.1.call-done
  125.2 0.0 all-gather.6.cloned.1.call-done
  125.2 0.0 copy-start.1
  125.2 0.0 copy-start.2
  125.3 0.0 copy-start.3
  125.3 10.9 %bitcast_dynamic-update-slice_fusion.4 = bf16[5,1,2048,1024]{3,2,1,0:T(8,128)(2,1)} fusion(bf16[1024,2048]{1,0:T(8,128)(2,1)} %all-gather.6.cloned.1.call-done, f32[1024]{0:T(1024)S(1)} %get-tuple-element.21, f32[1024]{0:T(1024)} %param.2, f32[2048]{0:T(1024)S(1)} %dynamic_slice.20, bf16[1024,1024]{1,0:T(8,128)(2,1)} %all-gather.8.cloned.1.call-done, ...), kind=kOutput, calls=%fused_computation.27 | convolution fusion | flops 4324327424 | bytes 10510336 | tf_op jit(solution)/shard_map/dot_general | solution.py:10
  136.1 0.0 copy-done.1
  136.1 7.8 bitcast_dynamic-update-slice_fusion.3
  143.9 7.4 bitcast_dynamic-update-slice_fusion.2
  151.3 6.9 bitcast_dynamic-update-slice_fusion.1
  158.2 6.8 bitcast_dynamic-update-slice_fusion
  165.0 23.9 %copy.21 = bf16[5,1,2048,1024]{3,0,1,2:T(8,128)(2,1)} copy(bf16[5,1,2048,1024]{3,2,1,0:T(8,128)(2,1)} %bitcast_dynamic-update-slice_fusion) | data formatting | bytes 41943040 | tf_op jit(solution)/shard_map/stack | solution.py:93
  189.0 9.9 all-to-all-start
  199.0 0.1 reshape.290
  199.1 0.1 copy.23
  199.2 0.5 broadcast.132
  199.8 1.1 slice_multiply_fusion.6
  200.8 0.1 mul.285
  200.9 0.1 squeeze.18
  201.0 0.1 bitcast_subtract_fusion
  201.0 0.1 maximum_reduce_fusion
  201.3 0.1 dynamic_slice.22
  201.3 0.1 copy_bitcast_fusion.1
  201.4 0.1 fusion.33
  201.5 715.7 %all-to-all-done = bf16[5,1,2048,1024]{3,0,1,2:T(8,128)(2,1)} async-done(((bf16[5,1,2048,1024]{3,0,1,2:T(8,128)(2,1)}), bf16[5,1,2048,1024]{3,0,1,2:T(8,128)(2,1)}, u32[]{:S(2)}, u32[]{:S(2)}) %all-to-all-start) | async-done | bytes 20971552 | tf_op jit(solution)/shard_map/all_to_all | solution.py:96
  917.2 26.6 %copy.22 = bf16[5,1,2048,1024]{3,2,0,1:T(8,128)(2,1)} copy(bf16[5,1,2048,1024]{3,0,1,2:T(8,128)(2,1)} %all-to-all-done) | data formatting | bytes 41943040 | tf_op jit(solution)/shard_map/all_to_all | solution.py:96
  943.9 16.0 %convert_reduce_fusion = f32[5,512,1024]{2,1,0:T(8,128)} fusion(bf16[5,4,512,1024]{3,2,1,0:T(8,128)(2,1)} %bitcast.61), kind=kLoop, calls=%fused_computation.1 | loop fusion | flops 18350080 | bytes 31457280 | tf_op jit(solution)/shard_map/reduce_sum | solution.py:98
  959.9 28.2 %convert_subtract_fusion = f32[5,4,512,1024]{3,2,1,0:T(8,128)} fusion(bf16[5,4,512,1024]{3,2,1,0:T(8,128)(2,1)} %bitcast.62, f32[5,512,1024]{2,1,0:T(8,128)} %convert_reduce_fusion), kind=kLoop, calls=%fused_computation | loop fusion | flops 20971520 | bytes 73400320 | tf_op jit(solution)/shard_map/sub | solution.py:99
  988.0 2.6 fusion.26
  990.6 20.2 %fusion.44 = (f32[512,1024]{1,0:T(8,128)S(1)}, f32[4,512,1024]{2,1,0:T(8,128)}) fusion(f32[4,1024]{1,0:T(4,128)S(1)} %bitcast.71, f32[4,512]{1,0:T(4,128)S(1)} %fusion.33, f32[5,4,512,1024]{3,2,1,0:T(8,128)} %convert_subtract_fusion), kind=kLoop, calls=%fused_computation.85 | loop fusion | flops 20447232 | bytes 52453376 | tf_op jit(solution)/shard_map/reduce_sum | solution.py:114
  1010.8 0.2 broadcast_multiply_fusion
  1010.9 5.1 multiply_reduce_fusion
  1016.0 0.5 multiply_sqrt_fusion
  1016.5 2.8 sqrt.22
  1019.3 3.0 div.75
  1022.4 2.6 rsqrt_multiply_fusion
  (23 shorter events, 0.3 us)
Async XLA Ops:
  7.2 118.0 %all-gather.8.cloned.1.call-start = ((), (), s32[]{:S(2)}) async-start(), calls=%async_computation.2 | async-start | bytes 3145728 | tf_op jit(solution)/shard_map/all_gather | solution.py:72
  7.9 117.3 %all-gather.6.cloned.1.call-start = ((), (), s32[]{:S(2)}) async-start(), calls=%async_computation.1 | async-start | bytes 5242880 | tf_op jit(solution)/shard_map/all_gather | solution.py:78
  125.2 10.9 %copy-start.1 = (f32[1024]{0:T(1024)S(1)}, f32[1024]{0:T(1024)}, u32[]{:S(2)}) copy-start(f32[1024]{0:T(1024)} %param.2) | copy-start | bytes 12292
  125.2 10.9 %copy-start.2 = (bf16[1024,2048]{1,0:T(8,128)(2,1)S(1)}, bf16[1024,2048]{1,0:T(8,128)(2,1)}, u32[]{:S(2)}) copy-start(bf16[1024,2048]{1,0:T(8,128)(2,1)} %all-gather.6.cloned.1.call-done) | copy-start | bytes 12582916
  125.3 10.9 %copy-start.3 = (bf16[1024,1024]{1,0:T(8,128)(2,1)S(1)}, bf16[1024,1024]{1,0:T(8,128)(2,1)}, u32[]{:S(2)}) copy-start(bf16[1024,1024]{1,0:T(8,128)(2,1)} %all-gather.8.cloned.1.call-done) | copy-start | bytes 6291460
  189.0 728.3 %all-to-all-start = ((bf16[5,1,2048,1024]{3,0,1,2:T(8,128)(2,1)}), bf16[5,1,2048,1024]{3,0,1,2:T(8,128)(2,1)}, u32[]{:S(2)}, u32[]{:S(2)}) async-start(bf16[5,1,2048,1024]{3,0,1,2:T(8,128)(2,1)} %copy.21), calls=%async_computation | async-start | bytes 67108864 | tf_op jit(solution)/shard_map/all_to_all | solution.py:96
  959.9 28.2 %copy-start = (f32[5,512,1024]{2,1,0:T(8,128)S(1)}, f32[5,512,1024]{2,1,0:T(8,128)}, u32[]{:S(2)}) copy-start(f32[5,512,1024]{2,1,0:T(8,128)} %convert_reduce_fusion) | copy-start | bytes 31457284
Sparse Core Ops, SparseCore 0:
  9.5 13.2 all-gather.7
  24.7 54.7 all-gather.5
where the time goes:
time: 1040 us; the launch traced here: 1030 us
  waiting for transfers between devices  717 us (69%)
  blocking collectives  109 us (10%)
  other arithmetic  81.7 us (8%)
  local copies, waits for them, and re-layouts  58.2 us (6%)
  matrix products  39.8 us (4%)
  between operations  16 us (2%)
    all_to_all x1, waiting for transfers between devices, per_device(): lax.all_to_all(sums, 'genome', split_axis=2, concat_axis=1, tiled=True)  716 us
    all_gather x1, blocking collectives, per_device(): lax.all_gather(own_stats[None], ('genome', 'trow', 'tcol'), axis=0, tiled...  67.2 us
    unnamed x1, blocking collectives  42.1 us
    dot_general x5, matrix products, contract(): lax.dot_general(left, right, (((0,), (0,)), ((), ())), preferred_element_...  39.8 us
    sub x1, other arithmetic, per_device(): deleted = totals[:, None] - tile_values  28.2 us
    all_to_all x1, local copies, waits for them, and re-layouts, per_device(): lax.all_to_all(sums, 'genome', split_axis=2, concat_axis=1, tiled=True)  26.6 us
    another operation x1, local copies, waits for them, and re-layouts, per_device(): sums = jnp.stack(products)  23.9 us
  transfers between devices with their start and end apart: 3, of which 1 were waited for; matrix products, arithmetic and copies ran while one was open for 1% of the time, Pallas kernels for 0%

commit v1 on v0

--- a/solution.py
+++ b/solution.py
@@ -1,14 +1,23 @@
+import functools
+
 import jax
 import jax.numpy as jnp
 from jax import lax
+from jax.experimental import pallas as pl
+from jax.experimental.pallas import tpu as pltpu
 from jax.sharding import PartitionSpec as P
 
 floor_value = 0.002
+axes = ("genome", "trow", "tcol")
+bf16 = jnp.bfloat16
+f32 = jnp.float32
+lanes = 128
+vmem_bytes = 56 << 20
 
 
 def contract(left, right):
     return lax.dot_general(
-        left, right, (((0,), (0,)), ((), ())), preferred_element_type=jnp.float32
+        left, right, (((0,), (0,)), ((), ())), preferred_element_type=f32
     )
 
 
@@ -17,14 +26,382 @@
 
 
 def weights_for(herit_pos, ld_column):
-    return (1.0 / (1.0 + herit_pos[None, :] * ld_column[:, None])).astype(jnp.bfloat16)
+    return (1.0 / (1.0 + herit_pos[None, :] * ld_column[:, None])).astype(bf16)
 
 
 def coupling(tiles):
     return (tiles[2] * tiles[1] - tiles[3] * tiles[0]) / (tiles[2] * tiles[4] - tiles[3] * tiles[3])
 
 
-def per_device(ldscore, zscores):
+def split_rows(value):
+    high = value.astype(bf16).astype(f32)
+    rest = value - high
+    middle = rest.astype(bf16).astype(f32)
+    return [high, middle, rest - middle]
+
+
+def down_sublanes(row):
+    return jnp.transpose(jnp.broadcast_to(row, (lanes, lanes)))
+
+
+def widen(column, width):
+    return jnp.concatenate([column] * (width // lanes), axis=1)
+
+
+def message_kernel(parts, idx, z_ref, ld_ref, ldrow_ref, *outs):
+    snps, width = z_ref.shape
+    piece = snps // parts
+    y_acc = jnp.zeros((8, width), f32)
+    l_acc = jnp.zeros((8, width), f32)
+    for chunk in range(snps // lanes):
+        weight = widen(down_sublanes(1.0 / ld_ref[chunk : chunk + 1, :]), width)
+        values = z_ref[chunk * lanes : (chunk + 1) * lanes, :].astype(f32)
+        square = values * values
+        l_acc = l_acc + jnp.sum(square.reshape(lanes // 8, 8, width), axis=0)
+        y_acc = y_acc + jnp.sum((square * weight).reshape(lanes // 8, 8, width), axis=0)
+    rows = split_rows(jnp.sum(y_acc, axis=0, keepdims=True))
+    rows = rows + split_rows(jnp.sum(l_acc, axis=0, keepdims=True))
+    rows = rows + split_rows(ldrow_ref[...])
+    tail = outs[0].shape[0] - piece
+    used = sum(row.shape[0] for row in rows)
+    rows = rows + [jnp.zeros((tail - used, width), f32)]
+    extra = jnp.concatenate(rows, axis=0).astype(bf16)
+    column = idx[2]
+    for step, out in enumerate(outs):
+        quarter = jnp.bitwise_xor(column, step)
+        out[:piece, :] = z_ref[pl.ds(pl.multiple_of(quarter * piece, piece), piece), :]
+        out[piece:, :] = extra
+
+
+def route_kernel(parts, idx, *refs):
+    ins, outs = refs[:parts], refs[parts:]
+    for shift in range(parts):
+        chosen = jnp.bitwise_xor(idx[2], lax.rem(idx[0] + shift, parts))
+        for step in range(parts):
+
+            @pl.when(chosen == step)
+            def _(shift=shift, step=step):
+                outs[shift][...] = ins[step][...]
+
+
+def join_kernel(parts, idx, *refs):
+    ins, (rows_ref, stat_ref, ld_ref) = refs[:parts], refs[parts:]
+    piece, width = rows_ref.shape[1:]
+    ld_rows = ld_ref.shape[0] // parts
+    for shift in range(parts):
+        block = lax.rem(idx[0] + parts - shift, parts)
+        rows_ref[block] = ins[shift][:piece, :]
+        extra = ins[shift][piece:, :].astype(f32)
+        stat_ref[pl.ds(block, 1), :] = (extra[2:3] + extra[1:2]) + extra[0:1]
+        stat_ref[pl.ds(parts + block, 1), :] = (extra[5:6] + extra[4:5]) + extra[3:4]
+        for row in range(ld_rows):
+            at = 6 + row
+            ld_ref[pl.ds(block * ld_rows + row, 1), :] = (
+                extra[at + 2 * ld_rows : at + 2 * ld_rows + 1]
+                + extra[at + ld_rows : at + ld_rows + 1]
+            ) + extra[at : at + 1]
+
+
+def total(values):
+    return jnp.sum(jnp.sum(values, axis=1, keepdims=True), axis=0, keepdims=True)
+
+
+def herit_full(stats, ld, blocks, snps):
+    inv = total(1.0 / ld)
+    return slope_fit(
+        inv,
+        total(ld),
+        jnp.sum(stats[:blocks], axis=0, keepdims=True),
+        jnp.sum(stats[blocks:], axis=0, keepdims=True),
+        float(snps * blocks),
+    )
+
+
+def herit_without(stats, ld, block, blocks, snps):
+    per = ld.shape[0] // blocks
+    inv = [total(1.0 / ld[b * per : (b + 1) * per]) for b in range(blocks)]
+    lds = [total(ld[b * per : (b + 1) * per]) for b in range(blocks)]
+    y_total = jnp.sum(stats[:blocks], axis=0, keepdims=True)
+    l_total = jnp.sum(stats[blocks:], axis=0, keepdims=True)
+    inv_total, ld_total = sum(inv[1:], inv[0]), sum(lds[1:], lds[0])
+    return slope_fit(
+        inv_total - inv[block],
+        ld_total - lds[block],
+        y_total - stats[block : block + 1],
+        l_total - stats[blocks + block : blocks + block + 1],
+        float(snps * (blocks - 1)),
+    )
+
+
+def weight_kernel(
+    blocks, idx, row_stat, own_stat, mate_stat, ld_ref, sums_ref, urow_ref, ucol_ref, ldcol_ref, inv_ref, wld_ref
+):
+    snps, width = urow_ref.shape
+    block = pl.program_id(0)
+    ld = ld_ref[...]
+    side = idx[1]
+    here = [pl.multiple_of(side * width, width), pl.multiple_of((1 - side) * width, width)]
+    herit_row = jnp.maximum(herit_full(row_stat[...], ld, blocks, snps), 0.0)
+    herit_col = [
+        jnp.maximum(herit_full(stat[...], ld, blocks, snps), 0.0) for stat in (own_stat, mate_stat)
+    ]
+    per = snps // width
+    step = width // lanes
+    row_of = lax.broadcasted_iota(jnp.int32, ld.shape, 0)
+    here_ld = [
+        jnp.sum(jnp.where(row_of == block * per + k, ld, 0.0), axis=0, keepdims=True) for k in range(per)
+    ]
+    for chunk in range(snps // lanes):
+        at = slice(chunk * lanes, (chunk + 1) * lanes)
+        column = down_sublanes(here_ld[chunk // step][:, (chunk % step) * lanes : (chunk % step + 1) * lanes])
+        ldcol_ref[at, :] = column
+        ld_wide = widen(column, width)
+        inv_wide = 1.0 / column
+        inv_wide = widen(inv_wide, width)
+        u_row = (1.0 / (1.0 + herit_row * ld_wide)).astype(bf16)
+        urow_ref[at, :] = u_row
+        u_float = u_row.astype(f32)
+        inv_ref[at, :] = (u_float * inv_wide).astype(bf16)
+        wld_ref[at, :] = (u_float * ld_wide).astype(bf16)
+        for half in range(2):
+            ucol_ref[at, pl.ds(here[half], width)] = (
+                1.0 / (1.0 + herit_col[half] * ld_wide)
+            ).astype(bf16)
+    u_col = ucol_ref[...]
+    sums_ref[0] = contract(inv_ref[...], u_col).astype(bf16)
+    sums_ref[1] = contract(urow_ref[...], u_col).astype(bf16)
+    sums_ref[2] = contract(wld_ref[...], u_col).astype(bf16)
+
+
+def pair_kernel(parts, idx, *refs):
+    pieces = refs[:parts]
+    own_ref, mate_ref, urow_ref, ucol_ref, ldcol_ref, out_ref, zu_ref, zinv_ref, zcol_ref = refs[parts:]
+    piece, width = pieces[0].shape
+    side = idx[1]
+    for half, ref in enumerate((own_ref, mate_ref)):
+        place = side if half == 0 else 1 - side
+        at = pl.ds(pl.multiple_of(place * width, width), width)
+        zcol_ref[:, at] = (ref[...].astype(f32) * ucol_ref[:, at].astype(f32)).astype(bf16)
+    for step in range(parts):
+        start = pl.multiple_of(jnp.bitwise_xor(idx[2], step) * piece, piece)
+        at = pl.ds(start, piece)
+        scaled = pieces[step][...].astype(f32) * urow_ref[at, :].astype(f32)
+        zu_ref[at, :] = scaled.astype(bf16)
+        zinv_ref[at, :] = (scaled * widen(1.0 / ldcol_ref[at, :], width)).astype(bf16)
+    z_col = zcol_ref[...]
+    out_ref[0] = contract(zinv_ref[...], z_col).astype(bf16)
+    out_ref[1] = contract(zu_ref[...], z_col).astype(bf16)
+
+
+def finish_kernel(blocks, snps, idx, row_stat, own_stat, mate_stat, ld_ref, w_ref, *refs):
+    pairs, (rg_ref, se_ref) = refs[:blocks], refs[blocks:]
+    tile = rg_ref.shape[1]
+    width = rg_ref.shape[3]
+    ld = ld_ref[...]
+    side = idx[1]
+    start = pl.multiple_of(pl.program_id(0) * tile, tile)
+
+    def scale(value):
+        return lax.rsqrt(jnp.maximum(value, floor_value))
+
+    def all_scales(ref):
+        stats = ref[...]
+        scales = [scale(herit_full(stats, ld, blocks, snps))]
+        return scales + [scale(herit_without(stats, ld, b, blocks, snps)) for b in range(blocks)]
+
+    row_scales = [down_sublanes(value) for value in all_scales_rows(row_stat, start, tile, ld, blocks, snps, scale)]
+    own, mate = all_scales(own_stat), all_scales(mate_stat)
+    for half in range(2):
+        col_scales = [jnp.where(side == half, a, b) for a, b in zip(own, mate)]
+        at = slice(half * width, (half + 1) * width)
+        y0 = [pairs[s][0, :, at].astype(f32) for s in range(blocks)]
+        y1 = [pairs[s][1, :, at].astype(f32) for s in range(blocks)]
+        block_of = [idx[3 + s] for s in range(blocks)]
+        w = [[w_ref[block_of[s], k, :, at].astype(f32) for s in range(blocks)] for k in range(3)]
+        tiles = [y0, y1] + w
+        sums = [sum(t[1:], t[0]) for t in tiles]
+        rg_ref[0, :, half, :] = coupling(sums) * (widen(row_scales[0], width) * col_scales[0])
+        dels = []
+        for s in range(blocks):
+            row_scale, col_scale = row_scales[1], col_scales[1]
+            for b in range(1, blocks):
+                row_scale = jnp.where(block_of[s] == b, row_scales[1 + b], row_scale)
+                col_scale = jnp.where(block_of[s] == b, col_scales[1 + b], col_scale)
+            rest = [total_ - t[s] for total_, t in zip(sums, tiles)]
+            dels.append(coupling(rest) * (widen(row_scale, width) * col_scale))
+        mean = sum(dels[1:], dels[0]) * (1.0 / blocks)
+        spread = sum([(d - mean) * (d - mean) for d in dels[1:]], (dels[0] - mean) * (dels[0] - mean))
+        se_ref[0, :, half, :] = jnp.sqrt((blocks - 1) / blocks * spread)
+
+
+def all_scales_rows(ref, start, tile, ld, blocks, snps, scale):
+    stats = ref[:, pl.ds(start, tile)]
+    scales = [scale(herit_full(stats, ld, blocks, snps))]
+    return scales + [scale(herit_without(stats, ld, b, blocks, snps)) for b in range(blocks)]
+
+
+def whole(shape):
+    return pl.BlockSpec(shape, lambda *_: (0,) * len(shape))
+
+
+def call(kernel, idx, ins, in_specs, outs, out_specs, grid=(1,), scratch=()):
+    return pl.pallas_call(
+        kernel,
+        grid_spec=pltpu.PrefetchScalarGridSpec(
+            num_scalar_prefetch=1,
+            grid=grid,
+            in_specs=in_specs,
+            out_specs=out_specs,
+            scratch_shapes=list(scratch),
+        ),
+        out_shape=outs,
+        compiler_params=pltpu.CompilerParams(vmem_limit_bytes=vmem_bytes),
+    )(idx, *ins)
+
+
+def square_device(sizes, ldscore, zscores):
+    blocks, grid_rows, parts = sizes
+    snps, width = zscores.shape
+    piece = snps // parts
+    g, r, c = (lax.axis_index(name) for name in axes)
+
+    def move(value, target):
+        pairs = []
+        for gi in range(blocks):
+            for ri in range(grid_rows):
+                for ci in range(parts):
+                    to = target(gi, ri, ci)
+                    if to is not None:
+                        source = (gi * grid_rows + ri) * parts + ci
+                        pairs.append((source, (to[0] * grid_rows + to[1]) * parts + to[2]))
+        return lax.ppermute(value, axes, pairs)
+
+    def swap(value):
+        return move(value, lambda gi, ri, ci: (gi, 1 - ri, ci))
+
+    def line(value, table):
+        return move(value, lambda gi, ri, ci: (table[gi], ri, ci) if gi in table else None)
+
+    low = g < 2
+    slot_blocks = [g, jnp.bitwise_xor(g, 1), jnp.where(low, 2, 1), jnp.where(low, 3, 0)]
+    idx = jnp.stack([g, r, c] + slot_blocks).astype(jnp.int32)
+
+    near = line(zscores, {0: 1, 1: 0, 2: 3, 3: 2})
+    inner = line(zscores, {1: 2, 2: 1})
+
+    ld_rows = snps // width
+    extra = -(-(6 + 3 * ld_rows) // 16) * 16
+    message = jax.ShapeDtypeStruct((piece + extra, width), bf16)
+    sent = call(
+        functools.partial(message_kernel, parts),
+        idx,
+        (zscores, ldscore.reshape(snps // lanes, lanes), ldscore.reshape(ld_rows, width)),
+        [whole((snps, width)), whole((snps // lanes, lanes)), whole((ld_rows, width))],
+        [message] * parts,
+        [whole(message.shape)] * parts,
+    )
+    held = [sent[0]] + [
+        move(sent[step], lambda gi, ri, ci, step=step: (gi, ri, ci ^ step)) for step in range(1, parts)
+    ]
+    routed = call(
+        functools.partial(route_kernel, parts),
+        idx,
+        held,
+        [whole(message.shape)] * parts,
+        [message] * parts,
+        [whole(message.shape)] * parts,
+    )
+    arrived = [routed[0]] + [
+        line(routed[step], {gi: (gi + step) % blocks for gi in range(blocks)}) for step in range(1, blocks)
+    ]
+    quarter_rows, row_stat, ld_all = call(
+        functools.partial(join_kernel, parts),
+        idx,
+        arrived,
+        [whole(message.shape)] * parts,
+        [
+            jax.ShapeDtypeStruct((blocks, piece, width), bf16),
+            jax.ShapeDtypeStruct((2 * blocks, width), f32),
+            jax.ShapeDtypeStruct((blocks * ld_rows, width), f32),
+        ],
+        [whole((blocks, piece, width)), whole((2 * blocks, width)), whole((blocks * ld_rows, width))],
+    )
+    own_stat = move(row_stat, lambda gi, ri, ci: (ci, ri, gi))
+    mate_stat = swap(own_stat)
+    rows = [quarter_rows] + [
+        move(quarter_rows, lambda gi, ri, ci, step=step: (gi, ri, ci ^ step)) for step in range(1, parts)
+    ]
+
+    outer = line(inner, {1: 0, 2: 3})
+    cross = line(near, {1: 2, 2: 1})
+    last = line(cross, {1: 0, 2: 3})
+    own = [zscores, near, inner + outer, cross + last]
+    mate = [swap(value) for value in own]
+
+    stat_spec = whole((2 * blocks, width))
+    ld_spec = whole((blocks * ld_rows, width))
+    wide = grid_rows * width
+    w_sums, u_row, u_col, ld_col = call(
+        functools.partial(weight_kernel, blocks),
+        idx,
+        (row_stat, own_stat, mate_stat, ld_all),
+        [stat_spec] * 3 + [ld_spec],
+        [
+            jax.ShapeDtypeStruct((blocks, 3, width, wide), bf16),
+            jax.ShapeDtypeStruct((blocks, snps, width), bf16),
+            jax.ShapeDtypeStruct((blocks, snps, wide), bf16),
+            jax.ShapeDtypeStruct((blocks, snps, lanes), f32),
+        ],
+        [
+            pl.BlockSpec((None, 3, width, wide), lambda b, _: (b, 0, 0, 0)),
+            pl.BlockSpec((None, snps, width), lambda b, _: (b, 0, 0)),
+            pl.BlockSpec((None, snps, wide), lambda b, _: (b, 0, 0)),
+            pl.BlockSpec((None, snps, lanes), lambda b, _: (b, 0, 0)),
+        ],
+        grid=(blocks,),
+        scratch=[pltpu.VMEM((snps, width), bf16)] * 2,
+    )
+    pairs = []
+    for slot in range(blocks):
+        pick = lambda i, ref, slot=slot: (ref[3 + slot], 0, 0)
+        pairs.append(
+            call(
+                functools.partial(pair_kernel, parts),
+                idx,
+                (*rows, own[slot], mate[slot], u_row, u_col, ld_col),
+                [pl.BlockSpec((None, piece, width), pick)] * parts
+                + [whole((snps, width))] * 2
+                + [
+                    pl.BlockSpec((None, snps, width), pick),
+                    pl.BlockSpec((None, snps, wide), pick),
+                    pl.BlockSpec((None, snps, lanes), pick),
+                ],
+                jax.ShapeDtypeStruct((2, width, wide), bf16),
+                whole((2, width, wide)),
+                scratch=[
+                    pltpu.VMEM((snps, width), bf16),
+                    pltpu.VMEM((snps, width), bf16),
+                    pltpu.VMEM((snps, wide), bf16),
+                ],
+            )
+        )
+    tile = lanes
+    out = jax.ShapeDtypeStruct((1, width, grid_rows, width), f32)
+    out_spec = pl.BlockSpec((1, tile, grid_rows, width), lambda i, _: (0, i, 0, 0))
+    return tuple(
+        call(
+            functools.partial(finish_kernel, blocks, snps),
+            idx,
+            (row_stat, own_stat, mate_stat, ld_all, w_sums, *pairs),
+            [stat_spec] * 3
+            + [ld_spec, pl.BlockSpec((blocks, 3, tile, wide), lambda i, _: (0, 0, i, 0))]
+            + [pl.BlockSpec((2, tile, wide), lambda i, _: (0, i, 0))] * blocks,
+            [out, out],
+            [out_spec, out_spec],
+            grid=(width // tile,),
+        )
+    )
+def general_device(ldscore, zscores):
     blocks = lax.axis_size("genome")
     grid_rows = lax.axis_size("trow")
     grid_cols = lax.axis_size("tcol")
@@ -120,6 +497,15 @@
 
 
 def solution(mesh):
+    sizes = tuple(mesh.shape[name] for name in axes)
+
+    def per_device(ldscore, zscores):
+        snps, width = zscores.shape
+        square = sizes[0] == sizes[2] == 4 and sizes[1] == 2 and width % lanes == 0
+        if square and snps % width == 0 and snps // sizes[2] % lanes == 0:
+            return square_device(sizes, ldscore, zscores)
+        return general_device(ldscore, zscores)
+
     return jax.shard_map(
         per_device,
         mesh=mesh,

time: 1040 us -> 208 us (0.20)
  waiting for transfers between devices: 717 us -> 83.6 us
  blocking collectives: 109 us -> 0 us
  Pallas kernels: 0 us -> 89.2 us
  other arithmetic: 81.7 us -> 3.71 us
  local copies, waits for them, and re-layouts: 58.2 us -> 5.79 us
  matrix products: 39.8 us -> 0 us
  between operations: 16 us -> 0.8 us
  starting transfers between devices: 10 us -> 24.6 us
    all_to_all x1 -> x0, waiting for transfers between devices: 716 us -> none  [per_device(): lax.all_to_all(sums, 'genome', split_axis=2, concat_axis=1, tiled=True)]
    pallas_call x0 -> x9, Pallas kernels: none -> 89.2 us  [call(): pl.pallas_call(kernel, grid_spec=pltpu.PrefetchScalarGridSpec(num_scalar_...]
    ppermute x0 -> x20, waiting for transfers between devices: none -> 83.6 us  [move(): return lax.ppermute(value, axes, pairs)]
    all_gather x1 -> x0, blocking collectives: 67.2 us -> none  [per_device(): lax.all_gather(own_stats[None], ('genome', 'trow', 'tcol'), axis=0, tiled...]
    reduce_sum x6 -> x0, other arithmetic: 44.2 us -> none  [the longest x1 20.2 us: per_device(): mean_del = jnp.mean(rg_del, axis=0)]
    unnamed x1 -> x0, blocking collectives: 42.1 us -> none
    dot_general x5 -> x0, matrix products: 39.8 us -> none  [contract(): lax.dot_general(left, right, (((0,), (0,)), ((), ())), preferred_element_...]
    sub x3 -> x0, other arithmetic: 28.2 us -> none  [the longest x1 28.2 us: per_device(): deleted = totals[:, None] - tile_values]
  transfers between devices with their start and end apart: 3 -> 20, of which waited for: 1 -> 8; matrix products, arithmetic and copies ran while one was open for 1% -> 3% of each run, Pallas kernels for 0% -> 28%
where the time goes in v1:
time: 208 us
  Pallas kernels  89.2 us (43%)
  waiting for transfers between devices  83.6 us (40%)
  starting transfers between devices  24.6 us (12%)
  local copies, waits for them, and re-layouts  5.79 us (3%)
  other arithmetic  3.71 us (2%)
    pallas_call x9, Pallas kernels, call(): pl.pallas_call(kernel, grid_spec=pltpu.PrefetchScalarGridSpec(num_scalar_...  89.2 us
    ppermute x20, waiting for transfers between devices, move(): return lax.ppermute(value, axes, pairs)  83.6 us
    ppermute x20, starting transfers between devices, move(): return lax.ppermute(value, axes, pairs)  24.6 us
  transfers between devices with their start and end apart: 20, of which 8 were waited for; matrix products, arithmetic and copies ran while one was open for 3% of the time, Pallas kernels for 28%

profile of v1, /device:TPU:0, one launch (start us, length us, event | category | flops | bytes accessed | tf_op | source)
XLA Modules:
  0.0 207.7 jit_solution(5751406532124471405)
XLA Ops:
  0.6 0.0 copy-start.5
  0.6 3.1 %collective-permute-start.12 = (bf16[1024,512]{1,0:T(8,128)(2,1)}, bf16[1024,512]{1,0:T(8,128)(2,1)S(1)}, u32[]{:S(2)}, u32[]{:S(2)}) collective-permute-start(bf16[1024,512]{1,0:T(8,128)(2,1)} %refs_4_.1), channel_id=1, source_target_pairs={{0,8},{1,9},{2,10},{3,11},{4,12},{5,13},{6,14},{7,15},{8,0},{9,1},... | collective-permute-start | bytes 3145736 | tf_op jit(solution)/shard_map/ppermute | solution.py:277
  3.8 1.6 collective-permute-start.14
  5.4 21.7 %collective-permute-done.12.refs_4_ = bf16[1024,512]{1,0:T(8,128)(2,1)S(1)} collective-permute-done((bf16[1024,512]{1,0:T(8,128)(2,1)}, bf16[1024,512]{1,0:T(8,128)(2,1)S(1)}, u32[]{:S(2)}, u32[]{:S(2)}) %collective-permute-start.12) | collective-permute-done | bytes 1048608 | tf_op jit(solution)/shard_map/ppermute | solution.py:277
  27.1 1.6 collective-permute-start.17
  28.8 1.3 reshape.11.ldrow_ref
  30.0 0.7 stack.28.idx
  30.7 3.3 %shard_map.41 = (bf16[272,512]{1,0:T(8,128)(2,1)}, bf16[272,512]{1,0:T(8,128)(2,1)}, bf16[272,512]{1,0:T(8,128)(2,1)}, bf16[272,512]{1,0:T(8,128)(2,1)}) custom-call(s32[7]{0:T(128)} %stack.28.idx, bf16[1024,512]{1,0:T(8,128)(2,1)} %refs_4_.1, f32[8,128]{1,0:T(8,128)} %bitcast.7, f32[2,512]{1,0:T(2,128)} %reshape.11.ldrow_ref), custom_call_target="tpu_custom_call" | custom-call | tf_op jit(solution)/shard_map/pallas_call | solution.py:248
  34.0 1.7 collective-permute-start
  35.6 1.5 collective-permute-start.1
  37.2 0.3 collective-permute-start.2
  37.5 6.2 %collective-permute-done.refs_1_ = bf16[272,512]{1,0:T(8,128)(2,1)S(1)} collective-permute-done((bf16[272,512]{1,0:T(8,128)(2,1)}, bf16[272,512]{1,0:T(8,128)(2,1)S(1)}, u32[]{:S(2)}, u32[]{:S(2)}) %collective-permute-start) | collective-permute-done | bytes 278560 | tf_op jit(solution)/shard_map/ppermute | solution.py:277
  43.7 5.4 %collective-permute-done.1.refs_2_ = bf16[272,512]{1,0:T(8,128)(2,1)S(1)} collective-permute-done((bf16[272,512]{1,0:T(8,128)(2,1)}, bf16[272,512]{1,0:T(8,128)(2,1)S(1)}, u32[]{:S(2)}, u32[]{:S(2)}) %collective-permute-start.1) | collective-permute-done | bytes 278560 | tf_op jit(solution)/shard_map/ppermute | solution.py:277
  49.1 0.7 copy-done.12
  49.8 0.1 copy-done.13
  49.9 3.0 %shard_map.42 = (bf16[272,512]{1,0:T(8,128)(2,1)}, bf16[272,512]{1,0:T(8,128)(2,1)}, bf16[272,512]{1,0:T(8,128)(2,1)}, bf16[272,512]{1,0:T(8,128)(2,1)}) custom-call(s32[7]{0:T(128)} %stack.28.idx, bf16[272,512]{1,0:T(8,128)(2,1)} %get-tuple-element.17.refs_0_, bf16[272,512]{1,0:T(8,128)(2,1)} %copy-done.11, bf16[272,512]{1,0:T(8,128)(2,1)} %copy-done.12, ...), custom_call_target="tpu_custom_call" | custom-call | tf_op jit(solution)/shard_map/pallas_call | solution.py:248
  52.9 3.3 %collective-permute-start.3 = (bf16[272,512]{1,0:T(8,128)(2,1)}, bf16[272,512]{1,0:T(8,128)(2,1)S(1)}, u32[]{:S(2)}, u32[]{:S(2)}) collective-permute-start(bf16[272,512]{1,0:T(8,128)(2,1)} %get-tuple-element.22), channel_id=1, source_target_pairs={{0,8},{1,9},{2,10},{3,11},{4,12},{5,13},{6,14},{7,15},{8,16},{9,17... | collective-permute-start | bytes 835592 | tf_op jit(solution)/shard_map/ppermute | solution.py:277
  56.2 0.9 collective-permute-start.4
  57.1 1.9 collective-permute-start.5
  59.0 1.3 collective-permute-start.15
  60.3 0.0 collective-permute-done.17
  60.3 1.3 collective-permute-start.18
  61.6 2.9 %collective-permute-done.3.refs_1_ = bf16[272,512]{1,0:T(8,128)(2,1)S(1)} collective-permute-done((bf16[272,512]{1,0:T(8,128)(2,1)}, bf16[272,512]{1,0:T(8,128)(2,1)S(1)}, u32[]{:S(2)}, u32[]{:S(2)}) %collective-permute-start.3) | collective-permute-done | bytes 278560 | tf_op jit(solution)/shard_map/ppermute | solution.py:277
  64.5 8.8 %collective-permute-done.4.refs_2_ = bf16[272,512]{1,0:T(8,128)(2,1)S(1)} collective-permute-done((bf16[272,512]{1,0:T(8,128)(2,1)}, bf16[272,512]{1,0:T(8,128)(2,1)S(1)}, u32[]{:S(2)}, u32[]{:S(2)}) %collective-permute-start.4) | collective-permute-done | bytes 278560 | tf_op jit(solution)/shard_map/ppermute | solution.py:277
  73.4 1.2 collective-permute-done.5.refs_3_
  74.6 0.7 copy-done.10
  75.3 2.9 %shard_map.43 = (bf16[4,256,512]{2,1,0:T(8,128)(2,1)}, f32[8,512]{1,0:T(8,128)}, f32[8,512]{1,0:T(8,128)}) custom-call(s32[7]{0:T(128)} %stack.28.idx, bf16[272,512]{1,0:T(8,128)(2,1)} %get-tuple-element.21.refs_0_, bf16[272,512]{1,0:T(8,128)(2,1)} %copy-done.8, bf16[272,512]{1,0:T(8,128)(2,1)} %copy-done.9, bf16[272,512]{1,0:T(8,128)(2,1)} %copy-done.10), custom_call_target="tpu_custom_call" | custom-call | tf_op jit(solution)/shard_map/pallas_call | solution.py:248
  78.2 1.5 collective-permute-start.10
  79.7 1.4 collective-permute-start.6
  81.1 16.7 %collective-permute-done.15 = bf16[1024,512]{1,0:T(8,128)(2,1)S(1)} collective-permute-done((bf16[1024,512]{1,0:T(8,128)(2,1)}, bf16[1024,512]{1,0:T(8,128)(2,1)S(1)}, u32[]{:S(2)}, u32[]{:S(2)}) %collective-permute-start.15) | collective-permute-done | bytes 1048608 | tf_op jit(solution)/shard_map/ppermute | solution.py:277
  97.7 0.8 collective-permute-start.9
  98.5 20.7 %collective-permute-done.18 = bf16[1024,512]{1,0:T(8,128)(2,1)} collective-permute-done((bf16[1024,512]{1,0:T(8,128)(2,1)}, bf16[1024,512]{1,0:T(8,128)(2,1)}, u32[]{:S(2)}, u32[]{:S(2)}) %collective-permute-start.18) | collective-permute-done | bytes 1048608 | tf_op jit(solution)/shard_map/ppermute | solution.py:277
  119.2 1.7 collective-permute-start.8
  120.9 1.5 add.6.refs_4_
  122.4 2.2 %add.7.refs_4_ = bf16[1024,512]{1,0:T(8,128)(2,1)S(1)} add(bf16[1024,512]{1,0:T(8,128)(2,1)} %collective-permute-done.17, bf16[1024,512]{1,0:T(8,128)(2,1)} %collective-permute-done.18) | non-fusion elementwise | flops 524288 | bytes 3145728 | tf_op jit(solution)/shard_map/add | solution.py:338
  124.7 0.2 collective-permute-start.13
  124.9 0.0 collective-permute-done.11.refs_5_
  124.9 0.4 collective-permute-start.16
  125.2 0.1 collective-permute-start.19
  125.4 21.2 %shard_map.44 = (bf16[4,3,512,1024]{3,2,1,0:T(8,128)(2,1)}, bf16[4,1024,512]{2,1,0:T(8,128)(2,1)}, bf16[4,1024,1024]{2,1,0:T(8,128)(2,1)}, f32[4,1024,128]{2,1,0:T(8,128)}) custom-call(s32[7]{0:T(128)} %stack.28.idx, f32[8,512]{1,0:T(8,128)} %get-tuple-element.25.row_stat, f32[8,512]{1,0:T(8,128)} %copy-done.14, f32[8,512]{1,0:T(8,128)} %copy-done.15, ...), custom_call_target="tpu_custom_call" | custom-call | tf_op jit(solution)/shard_map/pallas_call | solution.py:248
  146.7 0.9 copy-done.1
  147.6 0.3 copy-done.2
  147.9 9.0 %shard_map.45.refs_0_ = bf16[2,512,1024]{2,1,0:T(8,128)(2,1)} custom-call(s32[7]{0:T(128)} %stack.28.idx, bf16[4,256,512]{2,1,0:T(8,128)(2,1)} %get-tuple-element.28.refs_0_, bf16[4,256,512]{2,1,0:T(8,128)(2,1)} %copy-done.2, bf16[4,256,512]{2,1,0:T(8,128)(2,1)} %copy-done.1, bf16[4,256,512]{2,1,0:T(8,128)(2,1)} %copy-done, bf16[1024,512]{1,0:T(8,128)(2,1)} %refs_4_.1, ...), custom_call_target="tpu_custom_call" | custom-call | tf_op jit(solution)/shard_map/pallas_call | solution.py:248
  157.0 9.1 %shard_map.46.refs_1_ = bf16[2,512,1024]{2,1,0:T(8,128)(2,1)} custom-call(s32[7]{0:T(128)} %stack.28.idx, bf16[4,256,512]{2,1,0:T(8,128)(2,1)} %get-tuple-element.28.refs_0_, bf16[4,256,512]{2,1,0:T(8,128)(2,1)} %copy-done.2, bf16[4,256,512]{2,1,0:T(8,128)(2,1)} %copy-done.1, bf16[4,256,512]{2,1,0:T(8,128)(2,1)} %copy-done, bf16[1024,512]{1,0:T(8,128)(2,1)} %copy-done.6, ...), custom_call_target="tpu_custom_call" | custom-call | tf_op jit(solution)/shard_map/pallas_call | solution.py:248
  166.1 9.0 %shard_map.47.refs_2_ = bf16[2,512,1024]{2,1,0:T(8,128)(2,1)} custom-call(s32[7]{0:T(128)} %stack.28.idx, bf16[4,256,512]{2,1,0:T(8,128)(2,1)} %get-tuple-element.28.refs_0_, bf16[4,256,512]{2,1,0:T(8,128)(2,1)} %copy-done.2, bf16[4,256,512]{2,1,0:T(8,128)(2,1)} %copy-done.1, bf16[4,256,512]{2,1,0:T(8,128)(2,1)} %copy-done, bf16[1024,512]{1,0:T(8,128)(2,1)} %copy-done.4, ...), custom_call_target="tpu_custom_call" | custom-call | tf_op jit(solution)/shard_map/pallas_call | solution.py:248
  175.0 1.0 copy-done.7
  176.0 9.2 %shard_map.48.refs_3_ = bf16[2,512,1024]{2,1,0:T(8,128)(2,1)} custom-call(s32[7]{0:T(128)} %stack.28.idx, bf16[4,256,512]{2,1,0:T(8,128)(2,1)} %get-tuple-element.28.refs_0_, bf16[4,256,512]{2,1,0:T(8,128)(2,1)} %copy-done.2, bf16[4,256,512]{2,1,0:T(8,128)(2,1)} %copy-done.1, bf16[4,256,512]{2,1,0:T(8,128)(2,1)} %copy-done, bf16[1024,512]{1,0:T(8,128)(2,1)} %copy-done.3, ...), custom_call_target="tpu_custom_call" | custom-call | tf_op jit(solution)/shard_map/pallas_call | solution.py:248
  185.3 22.4 %shard_map.49 = (f32[1,512,2,512]{3,2,1,0:T(2,128)}, f32[1,512,2,512]{3,2,1,0:T(2,128)}) custom-call(s32[7]{0:T(128)} %stack.28.idx, f32[8,512]{1,0:T(8,128)} %get-tuple-element.25.row_stat, f32[8,512]{1,0:T(8,128)} %copy-done.14, f32[8,512]{1,0:T(8,128)} %copy-done.15, f32[8,512]{1,0:T(8,128)} %get-tuple-element.26.ld_ref, ...), custom_call_target="tpu_custom_call" | custom-call | tf_op jit(solution)/shard_map/pallas_call | solution.py:248
  (37 shorter events, 0.1 us)
Async XLA Ops:
  0.6 63.9 %copy-start.5 = (bf16[1024,512]{1,0:T(8,128)(2,1)S(1)}, bf16[1024,512]{1,0:T(8,128)(2,1)}, u32[]{:S(2)}) copy-start(bf16[1024,512]{1,0:T(8,128)(2,1)} %refs_4_.1) | copy-start | bytes 3145732
  0.6 26.5 %collective-permute-start.12 = (bf16[1024,512]{1,0:T(8,128)(2,1)}, bf16[1024,512]{1,0:T(8,128)(2,1)S(1)}, u32[]{:S(2)}, u32[]{:S(2)}) collective-permute-start(bf16[1024,512]{1,0:T(8,128)(2,1)} %refs_4_.1), channel_id=1, source_target_pairs={{0,8},{1,9},{2,10},{3,11},{4,12},{5,13},{6,14},{7,15},{8,0},{9,1},... | collective-permute-start | bytes 3145736 | tf_op jit(solution)/shard_map/ppermute | solution.py:277
  3.8 55.2 %collective-permute-start.14 = (bf16[1024,512]{1,0:T(8,128)(2,1)}, bf16[1024,512]{1,0:T(8,128)(2,1)}, u32[]{:S(2)}, u32[]{:S(2)}) collective-permute-start(bf16[1024,512]{1,0:T(8,128)(2,1)} %refs_4_.1), channel_id=1, source_target_pairs={{8,16},{9,17},{10,18},{11,19},{12,20},{13,21},{14,22},{15,23},{16,... | collective-permute-start | bytes 3145736 | tf_op jit(solution)/shard_map/ppermute | solution.py:277
  27.1 97.5 %copy-start.6 = (bf16[1024,512]{1,0:T(8,128)(2,1)}, bf16[1024,512]{1,0:T(8,128)(2,1)S(1)}, u32[]{:S(2)}) copy-start(bf16[1024,512]{1,0:T(8,128)(2,1)S(1)} %collective-permute-done.12.refs_4_) | copy-start | bytes 3145732
  27.1 33.2 %collective-permute-start.17 = (bf16[1024,512]{1,0:T(8,128)(2,1)S(1)}, bf16[1024,512]{1,0:T(8,128)(2,1)}, u32[]{:S(2)}, u32[]{:S(2)}) collective-permute-start(bf16[1024,512]{1,0:T(8,128)(2,1)S(1)} %collective-permute-done.12.refs_4_), channel_id=1, source_target_pairs={{8,16},{9,17},{10,18},{11,19},{12,20},{13,21},{14,22},{15,23},{16,... | collective-permute-start | bytes 3145736 | tf_op jit(solution)/shard_map/ppermute | solution.py:277
  34.0 9.7 %collective-permute-start = (bf16[272,512]{1,0:T(8,128)(2,1)}, bf16[272,512]{1,0:T(8,128)(2,1)S(1)}, u32[]{:S(2)}, u32[]{:S(2)}) collective-permute-start(bf16[272,512]{1,0:T(8,128)(2,1)} %get-tuple-element.18), channel_id=1, source_target_pairs={{0,1},{1,0},{2,3},{3,2},{4,5},{5,4},{6,7},{7,6},{8,9},{9,8},{10,11... | collective-permute-start | bytes 835592 | tf_op jit(solution)/shard_map/ppermute | solution.py:277
  35.6 13.4 %collective-permute-start.1 = (bf16[272,512]{1,0:T(8,128)(2,1)}, bf16[272,512]{1,0:T(8,128)(2,1)S(1)}, u32[]{:S(2)}, u32[]{:S(2)}) collective-permute-start(bf16[272,512]{1,0:T(8,128)(2,1)} %get-tuple-element.19), channel_id=1, source_target_pairs={{0,2},{1,3},{2,0},{3,1},{4,6},{5,7},{6,4},{7,5},{8,10},{9,11},{10,... | collective-permute-start | bytes 835592 | tf_op jit(solution)/shard_map/ppermute | solution.py:277
  37.2 11.9 %collective-permute-start.2 = (bf16[272,512]{1,0:T(8,128)(2,1)}, bf16[272,512]{1,0:T(8,128)(2,1)S(1)}, u32[]{:S(2)}, u32[]{:S(2)}) collective-permute-start(bf16[272,512]{1,0:T(8,128)(2,1)} %get-tuple-element.20), channel_id=1, source_target_pairs={{0,3},{1,2},{2,1},{3,0},{4,7},{5,6},{6,5},{7,4},{8,11},{9,10},{10,... | collective-permute-start | bytes 835592 | tf_op jit(solution)/shard_map/ppermute | solution.py:277
  43.7 5.4 %copy-start.11 = (bf16[272,512]{1,0:T(8,128)(2,1)}, bf16[272,512]{1,0:T(8,128)(2,1)S(1)}, u32[]{:S(2)}) copy-start(bf16[272,512]{1,0:T(8,128)(2,1)S(1)} %collective-permute-done.refs_1_) | copy-start | bytes 835588
  49.1 0.7 copy-start.12
  49.1 0.8 copy-start.13
  52.9 11.6 %collective-permute-start.3 = (bf16[272,512]{1,0:T(8,128)(2,1)}, bf16[272,512]{1,0:T(8,128)(2,1)S(1)}, u32[]{:S(2)}, u32[]{:S(2)}) collective-permute-start(bf16[272,512]{1,0:T(8,128)(2,1)} %get-tuple-element.22), channel_id=1, source_target_pairs={{0,8},{1,9},{2,10},{3,11},{4,12},{5,13},{6,14},{7,15},{8,16},{9,17... | collective-permute-start | bytes 835592 | tf_op jit(solution)/shard_map/ppermute | solution.py:277
  56.2 17.2 %collective-permute-start.4 = (bf16[272,512]{1,0:T(8,128)(2,1)}, bf16[272,512]{1,0:T(8,128)(2,1)S(1)}, u32[]{:S(2)}, u32[]{:S(2)}) collective-permute-start(bf16[272,512]{1,0:T(8,128)(2,1)} %get-tuple-element.23), channel_id=1, source_target_pairs={{0,16},{1,17},{2,18},{3,19},{4,20},{5,21},{6,22},{7,23},{8,24},{9,... | collective-permute-start | bytes 835592 | tf_op jit(solution)/shard_map/ppermute | solution.py:277
  57.1 17.5 %collective-permute-start.5 = (bf16[272,512]{1,0:T(8,128)(2,1)}, bf16[272,512]{1,0:T(8,128)(2,1)S(1)}, u32[]{:S(2)}, u32[]{:S(2)}) collective-permute-start(bf16[272,512]{1,0:T(8,128)(2,1)} %get-tuple-element.24), channel_id=1, source_target_pairs={{0,24},{1,25},{2,26},{3,27},{4,28},{5,29},{6,30},{7,31},{8,0},{9,1... | collective-permute-start | bytes 835592 | tf_op jit(solution)/shard_map/ppermute | solution.py:277
  59.0 38.7 %collective-permute-start.15 = (bf16[1024,512]{1,0:T(8,128)(2,1)}, bf16[1024,512]{1,0:T(8,128)(2,1)S(1)}, u32[]{:S(2)}, u32[]{:S(2)}) collective-permute-start(bf16[1024,512]{1,0:T(8,128)(2,1)} %collective-permute-done.14), channel_id=1, source_target_pairs={{8,0},{9,1},{10,2},{11,3},{12,4},{13,5},{14,6},{15,7},{16,24},{17,... | collective-permute-start | bytes 3145736 | tf_op jit(solution)/shard_map/ppermute | solution.py:277
  60.3 58.9 %collective-permute-start.18 = (bf16[1024,512]{1,0:T(8,128)(2,1)}, bf16[1024,512]{1,0:T(8,128)(2,1)}, u32[]{:S(2)}, u32[]{:S(2)}) collective-permute-start(bf16[1024,512]{1,0:T(8,128)(2,1)} %collective-permute-done.17), channel_id=1, source_target_pairs={{8,0},{9,1},{10,2},{11,3},{12,4},{13,5},{14,6},{15,7},{16,24},{17,... | collective-permute-start | bytes 3145736 | tf_op jit(solution)/shard_map/ppermute | solution.py:277
  64.5 10.0 %copy-start.8 = (bf16[272,512]{1,0:T(8,128)(2,1)}, bf16[272,512]{1,0:T(8,128)(2,1)S(1)}, u32[]{:S(2)}) copy-start(bf16[272,512]{1,0:T(8,128)(2,1)S(1)} %collective-permute-done.3.refs_1_) | copy-start | bytes 835588
  64.5 60.4 %collective-permute-start.11 = (bf16[1024,512]{1,0:T(8,128)(2,1)S(1)}, bf16[1024,512]{1,0:T(8,128)(2,1)}, u32[]{:S(2)}, u32[]{:S(2)}) collective-permute-start(bf16[1024,512]{1,0:T(8,128)(2,1)S(1)} %copy-done.5), channel_id=1, source_target_pairs={{0,4},{1,5},{2,6},{3,7},{4,0},{5,1},{6,2},{7,3},{8,12},{9,13},{10,... | collective-permute-start | bytes 3145736 | tf_op jit(solution)/shard_map/ppermute | solution.py:277
  73.3 1.2 copy-start.9
  74.5 0.7 copy-start.10
  78.2 47.1 %collective-permute-start.10 = (bf16[4,256,512]{2,1,0:T(8,128)(2,1)}, bf16[4,256,512]{2,1,0:T(8,128)(2,1)S(1)}, u32[]{:S(2)}, u32[]{:S(2)}) collective-permute-start(bf16[4,256,512]{2,1,0:T(8,128)(2,1)} %get-tuple-element.28.refs_0_), channel_id=1, source_target_pairs={{0,3},{1,2},{2,1},{3,0},{4,7},{5,6},{6,5},{7,4},{8,11},{9,10},{10,... | collective-permute-start | bytes 3145736 | tf_op jit(solution)/shard_map/ppermute | solution.py:277
  79.7 1.4 collective-permute-start.6
  81.0 43.6 %copy-start.14 = (f32[8,512]{1,0:T(8,128)}, f32[8,512]{1,0:T(8,128)S(1)}, u32[]{:S(2)}) copy-start(f32[8,512]{1,0:T(8,128)S(1)} %collective-permute-done.6.own_stat) | copy-start | bytes 49156
  81.0 43.6 %collective-permute-start.7 = (f32[8,512]{1,0:T(8,128)S(1)}, f32[8,512]{1,0:T(8,128)S(1)}, u32[]{:S(2)}, u32[]{:S(2)}) collective-permute-start(f32[8,512]{1,0:T(8,128)S(1)} %collective-permute-done.6.own_stat), channel_id=1, source_target_pairs={{0,4},{1,5},{2,6},{3,7},{4,0},{5,1},{6,2},{7,3},{8,12},{9,13},{10,... | collective-permute-start | bytes 49160 | tf_op jit(solution)/shard_map/ppermute | solution.py:277
  97.7 48.9 %collective-permute-start.9 = (bf16[4,256,512]{2,1,0:T(8,128)(2,1)}, bf16[4,256,512]{2,1,0:T(8,128)(2,1)S(1)}, u32[]{:S(2)}, u32[]{:S(2)}) collective-permute-start(bf16[4,256,512]{2,1,0:T(8,128)(2,1)} %get-tuple-element.28.refs_0_), channel_id=1, source_target_pairs={{0,2},{1,3},{2,0},{3,1},{4,6},{5,7},{6,4},{7,5},{8,10},{9,11},{10,... | collective-permute-start | bytes 3145736 | tf_op jit(solution)/shard_map/ppermute | solution.py:277
  119.2 27.5 %collective-permute-start.8 = (bf16[4,256,512]{2,1,0:T(8,128)(2,1)}, bf16[4,256,512]{2,1,0:T(8,128)(2,1)S(1)}, u32[]{:S(2)}, u32[]{:S(2)}) collective-permute-start(bf16[4,256,512]{2,1,0:T(8,128)(2,1)} %get-tuple-element.28.refs_0_), channel_id=1, source_target_pairs={{0,1},{1,0},{2,3},{3,2},{4,5},{5,4},{6,7},{7,6},{8,9},{9,8},{10,11... | collective-permute-start | bytes 3145736 | tf_op jit(solution)/shard_map/ppermute | solution.py:277
  122.4 34.6 %copy-start.4 = (bf16[1024,512]{1,0:T(8,128)(2,1)}, bf16[1024,512]{1,0:T(8,128)(2,1)S(1)}, u32[]{:S(2)}) copy-start(bf16[1024,512]{1,0:T(8,128)(2,1)S(1)} %add.6.refs_4_) | copy-start | bytes 3145732
  124.6 32.4 %copy-start.3 = (bf16[1024,512]{1,0:T(8,128)(2,1)}, bf16[1024,512]{1,0:T(8,128)(2,1)S(1)}, u32[]{:S(2)}) copy-start(bf16[1024,512]{1,0:T(8,128)(2,1)S(1)} %add.7.refs_4_) | copy-start | bytes 3145732
  124.6 0.7 copy-start.15
  124.7 32.3 %collective-permute-start.13 = (bf16[1024,512]{1,0:T(8,128)(2,1)S(1)}, bf16[1024,512]{1,0:T(8,128)(2,1)}, u32[]{:S(2)}, u32[]{:S(2)}) collective-permute-start(bf16[1024,512]{1,0:T(8,128)(2,1)S(1)} %collective-permute-done.12.refs_4_), channel_id=1, source_target_pairs={{0,4},{1,5},{2,6},{3,7},{4,0},{5,1},{6,2},{7,3},{8,12},{9,13},{10,... | collective-permute-start | bytes 3145736 | tf_op jit(solution)/shard_map/ppermute | solution.py:277
  124.9 41.2 %collective-permute-start.16 = (bf16[1024,512]{1,0:T(8,128)(2,1)S(1)}, bf16[1024,512]{1,0:T(8,128)(2,1)}, u32[]{:S(2)}, u32[]{:S(2)}) collective-permute-start(bf16[1024,512]{1,0:T(8,128)(2,1)S(1)} %add.6.refs_4_), channel_id=1, source_target_pairs={{0,4},{1,5},{2,6},{3,7},{4,0},{5,1},{6,2},{7,3},{8,12},{9,13},{10,... | collective-permute-start | bytes 3145736 | tf_op jit(solution)/shard_map/ppermute | solution.py:277
  125.2 21.4 %copy-start = (bf16[4,256,512]{2,1,0:T(8,128)(2,1)}, bf16[4,256,512]{2,1,0:T(8,128)(2,1)S(1)}, u32[]{:S(2)}) copy-start(bf16[4,256,512]{2,1,0:T(8,128)(2,1)S(1)} %collective-permute-done.10.refs_3_) | copy-start | bytes 3145732
  125.2 49.8 %collective-permute-start.19 = (bf16[1024,512]{1,0:T(8,128)(2,1)S(1)}, bf16[1024,512]{1,0:T(8,128)(2,1)S(1)}, u32[]{:S(2)}, u32[]{:S(2)}) collective-permute-start(bf16[1024,512]{1,0:T(8,128)(2,1)S(1)} %add.7.refs_4_), channel_id=1, source_target_pairs={{0,4},{1,5},{2,6},{3,7},{4,0},{5,1},{6,2},{7,3},{8,12},{9,13},{10,... | collective-permute-start | bytes 3145736 | tf_op jit(solution)/shard_map/ppermute | solution.py:277
  146.6 1.0 copy-start.1
  146.6 1.3 copy-start.2
  175.0 1.0 copy-start.7

commit v2 on v0

--- a/solution.py
+++ b/solution.py
@@ -1,14 +1,24 @@
+import functools
+
 import jax
 import jax.numpy as jnp
 from jax import lax
+from jax.experimental import pallas as pl
+from jax.experimental.pallas import tpu as pltpu
 from jax.sharding import PartitionSpec as P
 
+
 floor_value = 0.002
+axes = ("genome", "trow", "tcol")
+bf16 = jnp.bfloat16
+f32 = jnp.float32
+lanes = 128
+vmem_bytes = 56 << 20
 
 
 def contract(left, right):
     return lax.dot_general(
-        left, right, (((0,), (0,)), ((), ())), preferred_element_type=jnp.float32
+        left, right, (((0,), (0,)), ((), ())), preferred_element_type=f32
     )
 
 
@@ -17,14 +27,449 @@
 
 
 def weights_for(herit_pos, ld_column):
-    return (1.0 / (1.0 + herit_pos[None, :] * ld_column[:, None])).astype(jnp.bfloat16)
+    return (1.0 / (1.0 + herit_pos[None, :] * ld_column[:, None])).astype(bf16)
 
 
 def coupling(tiles):
     return (tiles[2] * tiles[1] - tiles[3] * tiles[0]) / (tiles[2] * tiles[4] - tiles[3] * tiles[3])
 
 
-def per_device(ldscore, zscores):
+def down_sublanes(row):
+    return jnp.transpose(jnp.broadcast_to(row, (lanes, lanes)))
+
+
+def widen(column, width):
+    return jnp.concatenate([column] * (width // lanes), axis=1)
+
+
+def message_kernel(parts, idx, z_ref, ld_ref, stat_ref, *outs):
+    snps, width = z_ref.shape
+    piece = width // parts
+    for step, out in enumerate(outs):
+        quarter = jnp.bitwise_xor(idx[2], step)
+        out[...] = z_ref[:, pl.ds(pl.multiple_of(quarter * piece, piece), piece)]
+    y_acc = jnp.zeros((8, width), f32)
+    l_acc = jnp.zeros((8, width), f32)
+    for chunk in range(snps // lanes):
+        weight = widen(down_sublanes(1.0 / ld_ref[chunk : chunk + 1, :]), width)
+        values = z_ref[chunk * lanes : (chunk + 1) * lanes, :].astype(f32)
+        square = values * values
+        l_acc = l_acc + jnp.sum(square.reshape(lanes // 8, 8, width), axis=0)
+        y_acc = y_acc + jnp.sum((square * weight).reshape(lanes // 8, 8, width), axis=0)
+    rows = [jnp.sum(y_acc, axis=0, keepdims=True), jnp.sum(l_acc, axis=0, keepdims=True)]
+    step = width // lanes
+    for row in range(snps // width):
+        rows.append(jnp.concatenate([ld_ref[row * step + k : row * step + k + 1, :] for k in range(step)], axis=1))
+    used = len(rows)
+    stat_ref[...] = jnp.concatenate(rows + [jnp.zeros((stat_ref.shape[0] - used, width), f32)], axis=0)
+
+
+def gather_kernel(parts, ld_rows, idx, *refs):
+    ins, cols, (stat_ref, own_ref, ld_ref) = refs[:parts], refs[parts : 2 * parts], refs[2 * parts :]
+    for step in range(parts):
+        for source, out_ref, place in ((ins, stat_ref, idx[2]), (cols, own_ref, idx[0])):
+            block = lax.rem(place + parts - step, parts)
+            out_ref[pl.ds(block, 1), :] = source[step][0:1, :]
+            out_ref[pl.ds(parts + block, 1), :] = source[step][1:2, :]
+        block = lax.rem(idx[2] + parts - step, parts)
+        for row in range(ld_rows):
+            ld_ref[pl.ds(block * ld_rows + row, 1), :] = ins[step][2 + row : 3 + row, :]
+
+
+def route_kernel(parts, idx, *refs):
+    ins, outs = refs[:parts], refs[parts:]
+    for shift in range(parts):
+        chosen = jnp.bitwise_xor(idx[2], lax.rem(idx[0] + shift, parts))
+        for step in range(parts):
+
+            @pl.when(chosen == step)
+            def _(shift=shift, step=step):
+                outs[shift][...] = ins[step][...]
+
+
+def join_kernel(idx, *refs):
+    ins, out_ref = refs[:-1], refs[-1]
+    for place, ref in enumerate(ins):
+        out_ref[place] = ref[...]
+
+
+def total(values):
+    return jnp.sum(jnp.sum(values, axis=1, keepdims=True), axis=0, keepdims=True)
+
+
+def herit_full(stats, ld, blocks, snps):
+    inv = total(1.0 / ld)
+    return slope_fit(
+        inv,
+        total(ld),
+        jnp.sum(stats[:blocks], axis=0, keepdims=True),
+        jnp.sum(stats[blocks:], axis=0, keepdims=True),
+        float(snps * blocks),
+    )
+
+
+def herit_without(stats, ld, block, blocks, snps):
+    per = ld.shape[0] // blocks
+    inv = [total(1.0 / ld[b * per : (b + 1) * per]) for b in range(blocks)]
+    lds = [total(ld[b * per : (b + 1) * per]) for b in range(blocks)]
+    y_total = jnp.sum(stats[:blocks], axis=0, keepdims=True)
+    l_total = jnp.sum(stats[blocks:], axis=0, keepdims=True)
+    inv_total, ld_total = sum(inv[1:], inv[0]), sum(lds[1:], lds[0])
+    return slope_fit(
+        inv_total - inv[block],
+        ld_total - lds[block],
+        y_total - stats[block : block + 1],
+        l_total - stats[blocks + block : blocks + block + 1],
+        float(snps * (blocks - 1)),
+    )
+
+
+def scale_of(herit):
+    return lax.rsqrt(jnp.maximum(herit, floor_value))
+
+
+def all_scales(stats, ld, blocks, snps):
+    scales = [scale_of(herit_full(stats, ld, blocks, snps))]
+    return scales + [scale_of(herit_without(stats, ld, b, blocks, snps)) for b in range(blocks)]
+
+
+def weight_kernel(blocks, begin, kept, idx, row_stat, own_stat, mate_stat, ld_ref, *refs):
+    sums_ref, urow_ref, ucol_ref, invcol_ref, inv_ref, wld_ref = refs[kept:]
+    snps, width = urow_ref.shape
+    block = idx[3 + begin + pl.program_id(0)]
+    ld = ld_ref[...]
+    side = idx[1]
+    here = [pl.multiple_of(side * width, width), pl.multiple_of((1 - side) * width, width)]
+    herit_row = jnp.maximum(herit_full(row_stat[...], ld, blocks, snps), 0.0)
+    herit_col = [
+        jnp.maximum(herit_full(stat[...], ld, blocks, snps), 0.0) for stat in (own_stat, mate_stat)
+    ]
+    per = snps // width
+    step = width // lanes
+    row_of = lax.broadcasted_iota(jnp.int32, ld.shape, 0)
+    here_ld = [
+        jnp.sum(jnp.where(row_of == block * per + k, ld, 0.0), axis=0, keepdims=True) for k in range(per)
+    ]
+    for chunk in range(snps // lanes):
+        at = slice(chunk * lanes, (chunk + 1) * lanes)
+        column = down_sublanes(here_ld[chunk // step][:, (chunk % step) * lanes : (chunk % step + 1) * lanes])
+        inv_column = 1.0 / column
+        invcol_ref[at, :] = inv_column
+        ld_wide = widen(column, width)
+        inv_wide = widen(inv_column, width)
+        u_row = (1.0 / (1.0 + herit_row * ld_wide)).astype(bf16)
+        urow_ref[at, :] = u_row
+        u_float = u_row.astype(f32)
+        inv_ref[at, :] = (u_float * inv_wide).astype(bf16)
+        wld_ref[at, :] = (u_float * ld_wide).astype(bf16)
+        for half in range(2):
+            ucol_ref[at, pl.ds(here[half], width)] = (
+                1.0 / (1.0 + herit_col[half] * ld_wide)
+            ).astype(bf16)
+    u_col = ucol_ref[...]
+    sums_ref[0] = contract(inv_ref[...], u_col).astype(bf16)
+    sums_ref[1] = contract(urow_ref[...], u_col).astype(bf16)
+    sums_ref[2] = contract(wld_ref[...], u_col).astype(bf16)
+
+
+def weigh_columns(side, own_ref, mate_ref, ucol, place_ref):
+    width = own_ref.shape[1]
+    for half, ref in enumerate((own_ref, mate_ref)):
+        place = side if half == 0 else 1 - side
+        at = pl.ds(pl.multiple_of(place * width, width), width)
+        place_ref[:, at] = ref[...] * ucol[:, at]
+
+
+def weigh_rows(rows, urow, invcol, zu_ref, zinv_ref):
+    snps, width = rows.shape
+    for chunk in range(snps // lanes):
+        at = slice(chunk * lanes, (chunk + 1) * lanes)
+        scaled = rows[at, :].astype(f32) * urow[at, :].astype(f32)
+        zu_ref[at, :] = scaled.astype(bf16)
+        zinv_ref[at, :] = (scaled * widen(invcol[at, :], width)).astype(bf16)
+
+
+def chosen(values, which):
+    picked = values[0]
+    for place in range(1, len(values)):
+        picked = jnp.where(which == place, values[place], picked)
+    return picked
+
+
+def finish_kernel(parts, blocks, idx, *refs):
+    first, pieces, refs = refs[:parts], refs[parts : 2 * parts], refs[2 * parts :]
+    own, mate, refs = refs[:blocks], refs[blocks : 2 * blocks], refs[2 * blocks :]
+    urow_hbm, ucol_hbm, inv_hbm, w_hbm, row_stat, own_stat, mate_stat, ld_ref, rg_ref, se_ref = refs[:10]
+    rows_v, own_v, mate_v, urow_v, ucol_v, inv_v, zu_v, zinv_v, zcol_v, y_v, w_v, rs_v, cs_v, sems, w_sem = refs[10:]
+    piece = first[0].shape[1]
+    tile, width = rg_ref.shape[1], rg_ref.shape[3]
+    snps = own[0].shape[0]
+    side = idx[1]
+    step_id = pl.program_id(0)
+    w_copy = pltpu.make_async_copy(w_hbm, w_v, w_sem.at[0])
+
+    @pl.when(step_id == 0)
+    def _():
+        copies = []
+        for slot in range(blocks):
+            turn = slot % 2
+            mine = [
+                (ucol_hbm.at[slot], ucol_v.at[turn]),
+                (own[slot], own_v.at[turn]),
+                (mate[slot], mate_v.at[turn]),
+                (urow_hbm.at[slot], urow_v.at[turn]),
+                (inv_hbm.at[slot], inv_v.at[turn]),
+            ]
+            for step in range(parts):
+                start = pl.multiple_of(jnp.bitwise_xor(idx[2], step) * piece, piece)
+                source = pieces[step].at[idx[3 + parts + slot]] if slot else first[step]
+                mine.append((source, rows_v.at[turn, :, pl.ds(start, piece)]))
+            copies.append([pltpu.make_async_copy(p, q, sems.at[slot, k]) for k, (p, q) in enumerate(mine)])
+
+        def load(slot):
+            if slot < blocks:
+                for copy in copies[slot]:
+                    copy.start()
+
+        def prepare(slot):
+            if slot < blocks:
+                for copy in copies[slot]:
+                    copy.wait()
+                turn = slot % 2
+                weigh_columns(side, own_v.at[turn], mate_v.at[turn], ucol_v.at[turn], zcol_v.at[turn])
+                weigh_rows(rows_v.at[turn], urow_v.at[turn], inv_v.at[turn], zu_v.at[turn], zinv_v.at[turn])
+                load(slot + 2)
+                if slot == 1:
+                    w_copy.start()
+
+        load(0)
+        load(1)
+        ld = ld_ref[...]
+
+        def scales(stat):
+            values = all_scales(stat[...], ld, blocks, snps)
+            return values[:1] + [chosen(values[1:], idx[3 + slot]) for slot in range(blocks)]
+
+        for place, value in enumerate(scales(row_stat)):
+            for chunk in range(width // lanes):
+                rs_v[place, chunk * lanes : (chunk + 1) * lanes, :] = down_sublanes(
+                    value[:, chunk * lanes : (chunk + 1) * lanes]
+                )
+        for place, (p, q) in enumerate(zip(scales(own_stat), scales(mate_stat))):
+            cs_v[place : place + 1, :width] = jnp.where(side == 0, p, q)
+            cs_v[place : place + 1, width:] = jnp.where(side == 0, q, p)
+        prepare(0)
+        for slot in range(blocks):
+            prepare(slot + 1)
+            turn = slot % 2
+            z_col = zcol_v[turn]
+            y_v[slot, 0] = contract(zinv_v[turn], z_col).astype(bf16)
+            y_v[slot, 1] = contract(zu_v[turn], z_col).astype(bf16)
+
+    @pl.when(step_id == 1)
+    def _():
+        w_copy.wait()
+
+    @pl.when(step_id > 0)
+    def _():
+        start = pl.multiple_of((step_id - 1) * tile, tile)
+        here = pl.ds(start, tile)
+        for group in range(2 * width // lanes):
+            at = slice(group * lanes, (group + 1) * lanes)
+            half, inner = divmod(group * lanes, width)
+            place = slice(inner, inner + lanes)
+            t = [[y_v[s, k, here, at].astype(f32) for s in range(blocks)] for k in range(2)]
+            t += [[w_v[s, k, here, at].astype(f32) for s in range(blocks)] for k in range(3)]
+            sums = [sum(x[1:], x[0]) for x in t]
+            values = []
+            for s in range(blocks + 1):
+                tiles = sums if s == 0 else [total_ - x[s - 1] for total_, x in zip(sums, t)]
+                values.append(coupling(tiles) * (rs_v[s, here, :] * cs_v[s : s + 1, at]))
+            rg_ref[0, :, half, place] = values[0]
+            dels = values[1:]
+            mean = sum(dels[1:], dels[0]) * (1.0 / blocks)
+            spread = sum([(d - mean) * (d - mean) for d in dels[1:]], (dels[0] - mean) * (dels[0] - mean))
+            se_ref[0, :, half, place] = jnp.sqrt((blocks - 1) / blocks * spread)
+
+
+def whole(shape):
+    return pl.BlockSpec(shape, lambda *_: (0,) * len(shape))
+
+
+def call(kernel, idx, ins, in_specs, outs, out_specs, grid=(1,), scratch=(), flops=0, ops=0, aliases={}):
+    moved = sum(x.size * x.dtype.itemsize for x in jax.tree.leaves((ins, outs)))
+    return pl.pallas_call(
+        kernel,
+        input_output_aliases=aliases,
+        grid_spec=pltpu.PrefetchScalarGridSpec(
+            num_scalar_prefetch=1,
+            grid=grid,
+            in_specs=in_specs,
+            out_specs=out_specs,
+            scratch_shapes=list(scratch),
+        ),
+        out_shape=outs,
+        compiler_params=pltpu.CompilerParams(vmem_limit_bytes=vmem_bytes),
+        cost_estimate=pl.CostEstimate(flops=flops, transcendentals=ops, bytes_accessed=moved),
+    )(idx, *ins)
+
+
+def square_device(sizes, ldscore, zscores):
+    blocks, grid_rows, parts = sizes
+    snps, width = zscores.shape
+    piece = width // parts
+    g, r, c = (lax.axis_index(name) for name in axes)
+
+    def move(value, target):
+        pairs = []
+        for gi in range(blocks):
+            for ri in range(grid_rows):
+                for ci in range(parts):
+                    to = target(gi, ri, ci)
+                    if to is not None:
+                        source = (gi * grid_rows + ri) * parts + ci
+                        pairs.append((source, (to[0] * grid_rows + to[1]) * parts + to[2]))
+        return lax.ppermute(value, axes, pairs)
+
+    def swap(value):
+        return move(value, lambda gi, ri, ci: (gi, 1 - ri, ci))
+
+    def line(value, table):
+        return move(value, lambda gi, ri, ci: (table[gi], ri, ci) if gi in table else None)
+
+    low = g < 2
+    slot_blocks = [g, jnp.bitwise_xor(g, 1), jnp.where(low, 2, 1), jnp.where(low, 3, 0)]
+    shifts = [lax.rem(g + blocks - b, blocks) - 1 for b in slot_blocks]
+    idx = jnp.stack([g, r, c] + slot_blocks + shifts).astype(jnp.int32)
+
+    near = line(zscores, {0: 1, 1: 0, 2: 3, 3: 2})
+    inner = line(zscores, {1: 2, 2: 1})
+
+    ld_rows = snps // width
+    message = jax.ShapeDtypeStruct((snps, piece), bf16)
+    note = jax.ShapeDtypeStruct((-(-(2 + ld_rows) // 8) * 8, width), f32)
+    stat = jax.ShapeDtypeStruct((2 * blocks, width), f32)
+    ld_shape = jax.ShapeDtypeStruct((blocks * ld_rows, width), f32)
+    notes, *sent = call(
+        functools.partial(message_kernel, parts),
+        idx,
+        (zscores, ldscore.reshape(snps // lanes, lanes)),
+        [whole((snps, width)), whole((snps // lanes, lanes))],
+        [note] + [message] * parts,
+        [whole(note.shape)] + [whole(message.shape)] * parts,
+    )
+    told = [move(notes, lambda gi, ri, ci, step=step: (ci, ri, (gi + step) % parts)) for step in range(parts)]
+    seen = [notes] + [line(notes, {gi: (gi + step) % blocks for gi in range(blocks)}) for step in range(1, blocks)]
+    held = [sent[0]] + [move(sent[step], lambda gi, ri, ci, step=step: (gi, ri, ci ^ step)) for step in range(1, parts)]
+    row_stat, own_stat, ld_all = call(
+        functools.partial(gather_kernel, parts, ld_rows),
+        idx,
+        (*told, *seen),
+        [whole(note.shape)] * (2 * parts),
+        [stat, stat, ld_shape],
+        [whole(stat.shape), whole(stat.shape), whole(ld_shape.shape)],
+    )
+    mate_stat = swap(own_stat)
+    routed = call(
+        functools.partial(route_kernel, parts),
+        idx,
+        held,
+        [whole(message.shape)] * parts,
+        [message] * parts,
+        [whole(message.shape)] * parts,
+    )
+    arrived = [line(routed[step], {gi: (gi + step) % blocks for gi in range(blocks)}) for step in range(1, blocks)]
+    first = [routed[0]] + [
+        move(routed[0], lambda gi, ri, ci, step=step: (gi, ri, ci ^ step)) for step in range(1, parts)
+    ]
+    joined = jax.ShapeDtypeStruct((blocks - 1, snps, piece), bf16)
+    quarter_rows = call(
+        join_kernel, idx, arrived, [whole(message.shape)] * (blocks - 1), joined, whole(joined.shape)
+    )
+    rows = [quarter_rows] + [
+        move(quarter_rows, lambda gi, ri, ci, step=step: (gi, ri, ci ^ step)) for step in range(1, parts)
+    ]
+    stats = (row_stat, own_stat, mate_stat, ld_all)
+    outer = line(inner, {1: 0, 2: 3})
+    half = snps // 2
+    cross = [line(near[k * half : (k + 1) * half], {1: 2, 2: 1}) for k in range(2)]
+    last = [line(cross[k], {1: 0, 2: 3}) for k in range(2)]
+    mate = [swap(zscores), swap(near)]
+
+    stat_spec = whole(stat.shape)
+    ld_spec = whole(ld_shape.shape)
+    wide = grid_rows * width
+    tile = lanes
+    anyspec = pl.BlockSpec(memory_space=pl.ANY)
+    stats = (row_stat, own_stat, mate_stat, ld_all)
+    stat_specs = [stat_spec] * 3 + [ld_spec]
+    held_weights = ()
+    span = blocks // 2
+    for k in range(2):
+        kept = len(held_weights)
+        spot = lambda i, _, k=k: (i + k * span, 0, 0)
+        held_weights = call(
+            functools.partial(weight_kernel, blocks, k * span, kept),
+            idx,
+            (*stats, *held_weights),
+            stat_specs + [anyspec] * kept,
+            [
+                jax.ShapeDtypeStruct((blocks, 3, width, wide), bf16),
+                jax.ShapeDtypeStruct((blocks, snps, width), bf16),
+                jax.ShapeDtypeStruct((blocks, snps, wide), bf16),
+                jax.ShapeDtypeStruct((blocks, snps, lanes), f32),
+            ],
+            [
+                pl.BlockSpec((None, 3, width, wide), lambda i, _, k=k: (i + k * span, 0, 0, 0)),
+                pl.BlockSpec((None, snps, width), spot),
+                pl.BlockSpec((None, snps, wide), spot),
+                pl.BlockSpec((None, snps, lanes), spot),
+            ],
+            grid=(span,),
+            scratch=[pltpu.VMEM((snps, width), bf16)] * 2,
+            flops=6 * span * snps * width * wide,
+            aliases={5 + j: j for j in range(kept)},
+        )
+    w_sums, u_row, u_col, inv_col = held_weights
+    outer, last[1], u_row = lax.optimization_barrier((outer, last[1], u_row))
+    own = [zscores, near, inner + outer]
+    own.append(jnp.concatenate([cross[k] + last[k] for k in range(2)], axis=0))
+    mate = mate + [swap(own[slot]) for slot in (2, 3)]
+    small = tile // 2
+    out = jax.ShapeDtypeStruct((1, width, grid_rows, width), f32)
+    out_spec = pl.BlockSpec((1, small, grid_rows, width), lambda i, _: (0, jnp.maximum(i - 1, 0), 0, 0))
+    return tuple(
+        call(
+            functools.partial(finish_kernel, parts, blocks),
+            idx,
+            (*first, *rows, *own, *mate, u_row, u_col, inv_col, w_sums, *stats),
+            [anyspec] * (2 * parts + 2 * blocks + 4) + stat_specs,
+            [out, out],
+            [out_spec, out_spec],
+            grid=(1 + width // small,),
+            scratch=[
+                pltpu.VMEM((2, snps, width), bf16),
+                pltpu.VMEM((2, snps, width), bf16),
+                pltpu.VMEM((2, snps, width), bf16),
+                pltpu.VMEM((2, snps, width), bf16),
+                pltpu.VMEM((2, snps, wide), bf16),
+                pltpu.VMEM((2, snps, lanes), f32),
+                pltpu.VMEM((2, snps, width), bf16),
+                pltpu.VMEM((2, snps, width), bf16),
+                pltpu.VMEM((2, snps, wide), bf16),
+                pltpu.VMEM((blocks, 2, width, wide), bf16),
+                pltpu.VMEM((blocks, 3, width, wide), bf16),
+                pltpu.VMEM((blocks + 1, width, lanes), f32),
+                pltpu.VMEM((8, wide), f32),
+                pltpu.SemaphoreType.DMA((blocks, 5 + parts)),
+                pltpu.SemaphoreType.DMA((1,)),
+            ],
+            flops=4 * blocks * snps * width * wide,
+        )
+    )
+
+
+def general_device(ldscore, zscores):
     blocks = lax.axis_size("genome")
     grid_rows = lax.axis_size("trow")
     grid_cols = lax.axis_size("tcol")
@@ -119,11 +564,24 @@
     return (rg_tile.reshape(out_shape), se_tile.reshape(out_shape))
 
 
+def is_square(sizes):
+    return sizes[0] == sizes[2] == 4 and sizes[1] == 2
+
+
 def solution(mesh):
-    return jax.shard_map(
+    sizes = tuple(mesh.shape[name] for name in axes)
+
+    def per_device(ldscore, zscores):
+        snps, width = zscores.shape
+        if is_square(sizes) and width % lanes == 0 and snps % width == 0 and width // sizes[2] % lanes == 0 and snps % (2 * lanes) == 0:
+            return square_device(sizes, ldscore, zscores)
+        return general_device(ldscore, zscores)
+
+    step = jax.shard_map(
         per_device,
         mesh=mesh,
         in_specs=(P("genome"), P("genome", ("trow", "tcol"))),
         out_specs=(P("trow", "genome", None, "tcol"), P("trow", "genome", None, "tcol")),
         check_vma=False,
     )
+    return step if is_square(sizes) else step

time: 1040 us -> 201 us (0.19)
  waiting for transfers between devices: 717 us -> 69.3 us
  blocking collectives: 109 us -> 0 us
  other arithmetic: 81.7 us -> 0.62 us
  Pallas kernels: 0 us -> 66.3 us
  local copies, waits for them, and re-layouts: 58.2 us -> 4.21 us
  starting transfers between devices: 10 us -> 58.1 us
  matrix products: 39.8 us -> 0 us
  between operations: 16 us -> 1.26 us
    all_to_all x1 -> x0, waiting for transfers between devices: 716 us -> none  [per_device(): lax.all_to_all(sums, 'genome', split_axis=2, concat_axis=1, tiled=True)]
    ppermute x0 -> x31, waiting for transfers between devices: none -> 69.3 us  [move(): return lax.ppermute(value, axes, pairs)]
    all_gather x1 -> x0, blocking collectives: 67.2 us -> none  [per_device(): lax.all_gather(own_stats[None], ('genome', 'trow', 'tcol'), axis=0, tiled...]
    pallas_call x0 -> x7, Pallas kernels: none -> 66.3 us  [call(): pl.pallas_call(kernel, input_output_aliases=aliases, grid_spec=pltpu.Pref...]
    ppermute x0 -> x31, starting transfers between devices: none -> 58.1 us  [move(): return lax.ppermute(value, axes, pairs)]
    reduce_sum x6 -> x0, other arithmetic: 44.2 us -> none  [the longest x1 20.2 us: per_device(): mean_del = jnp.mean(rg_del, axis=0)]
    unnamed x1 -> x0, blocking collectives: 42.1 us -> none
    dot_general x5 -> x0, matrix products: 39.8 us -> none  [contract(): lax.dot_general(left, right, (((0,), (0,)), ((), ())), preferred_element_...]
  transfers between devices with their start and end apart: 3 -> 31, of which waited for: 1 -> 7; matrix products, arithmetic and copies ran while one was open for 1% -> 1% of each run, Pallas kernels for 0% -> 18%
where the time goes in v2:
time: 201 us; the launch traced here: 200 us
  waiting for transfers between devices  69.3 us (34%)
  Pallas kernels  66.3 us (33%)
  starting transfers between devices  58.1 us (29%)
  local copies, waits for them, and re-layouts  4.21 us (2%)
    ppermute x31, waiting for transfers between devices, move(): return lax.ppermute(value, axes, pairs)  69.3 us
    pallas_call x7, Pallas kernels, call(): pl.pallas_call(kernel, input_output_aliases=aliases, grid_spec=pltpu.Pref...  66.3 us
    ppermute x31, starting transfers between devices, move(): return lax.ppermute(value, axes, pairs)  58.1 us
  transfers between devices with their start and end apart: 31, of which 7 were waited for; matrix products, arithmetic and copies ran while one was open for 1% of the time, Pallas kernels for 18%

profile of v2, /device:TPU:0, one launch (start us, length us, event | category | flops | bytes accessed | tf_op | source)
XLA Modules:
  0.0 199.8 jit_solution(11082733401441722043)
XLA Ops:
  0.6 3.1 %collective-permute-start.12 = (bf16[1024,512]{1,0:T(8,128)(2,1)}, bf16[1024,512]{1,0:T(8,128)(2,1)S(1)}, u32[]{:S(2)}, u32[]{:S(2)}) collective-permute-start(bf16[1024,512]{1,0:T(8,128)(2,1)} %refs_8_.1), channel_id=1, source_target_pairs={{0,8},{1,9},{2,10},{3,11},{4,12},{5,13},{6,14},{7,15},{8,0},{9,1},... | collective-permute-start | bytes 3145736 | tf_op jit(solution)/shard_map/ppermute | solution.py:332
  3.7 0.7 collective-permute-start.13
  4.5 0.6 stack.41.idx
  5.1 3.3 %shard_map.41 = (f32[8,512]{1,0:T(8,128)}, bf16[1024,128]{1,0:T(8,128)(2,1)}, bf16[1024,128]{1,0:T(8,128)(2,1)}, bf16[1024,128]{1,0:T(8,128)(2,1)}, bf16[1024,128]{1,0:T(8,128)(2,1)}) custom-call(s32[11]{0:T(128)} %stack.41.idx, bf16[1024,512]{1,0:T(8,128)(2,1)} %refs_8_.1, f32[8,128]{1,0:T(8,128)} %bitcast.10), custom_call_target="tpu_custom_call" | custom-call | bytes 2117632 | tf_op jit(solution)/shard_map/pallas_call | solution.py:301
  8.4 1.4 collective-permute-start.17
  9.8 6.4 %collective-permute-start.18 = (f32[8,512]{1,0:T(8,128)}, f32[8,512]{1,0:T(8,128)S(1)}, u32[]{:S(2)}, u32[]{:S(2)}) collective-permute-start(f32[8,512]{1,0:T(8,128)} %get-tuple-element.33.refs_4_), channel_id=1, source_target_pairs={{0,1},{1,9},{2,17},{3,25},{4,5},{5,13},{6,21},{7,29},{8,2},{9,10},... | collective-permute-start | bytes 49160 | tf_op jit(solution)/shard_map/ppermute | solution.py:332
  16.2 3.3 %collective-permute-start.19 = (f32[8,512]{1,0:T(8,128)}, f32[8,512]{1,0:T(8,128)S(1)}, u32[]{:S(2)}, u32[]{:S(2)}) collective-permute-start(f32[8,512]{1,0:T(8,128)} %get-tuple-element.33.refs_4_), channel_id=1, source_target_pairs={{0,2},{1,10},{2,18},{3,26},{4,6},{5,14},{6,22},{7,30},{8,3},{9,11}... | collective-permute-start | bytes 49160 | tf_op jit(solution)/shard_map/ppermute | solution.py:332
  19.5 13.1 %collective-permute-start.20 = (f32[8,512]{1,0:T(8,128)}, f32[8,512]{1,0:T(8,128)S(1)}, u32[]{:S(2)}, u32[]{:S(2)}) collective-permute-start(f32[8,512]{1,0:T(8,128)} %get-tuple-element.33.refs_4_), channel_id=1, source_target_pairs={{0,3},{1,11},{2,19},{3,27},{4,7},{5,15},{6,23},{7,31},{8,0},{9,8},... | collective-permute-start | bytes 49160 | tf_op jit(solution)/shard_map/ppermute | solution.py:332
  32.6 1.0 collective-permute-done.19.refs_2_
  33.6 4.9 %collective-permute-start.22 = (f32[8,512]{1,0:T(8,128)}, f32[8,512]{1,0:T(8,128)S(1)}, u32[]{:S(2)}, u32[]{:S(2)}) collective-permute-start(f32[8,512]{1,0:T(8,128)} %get-tuple-element.33.refs_4_), channel_id=1, source_target_pairs={{0,16},{1,17},{2,18},{3,19},{4,20},{5,21},{6,22},{7,23},{8,24},{9,... | collective-permute-start | bytes 49160 | tf_op jit(solution)/shard_map/ppermute | solution.py:332
  38.6 1.5 collective-permute-start.23
  40.1 3.5 %collective-permute-start = (bf16[1024,128]{1,0:T(8,128)(2,1)}, bf16[1024,128]{1,0:T(8,128)(2,1)S(1)}, u32[]{:S(2)}, u32[]{:S(2)}) collective-permute-start(bf16[1024,128]{1,0:T(8,128)(2,1)} %get-tuple-element.26), channel_id=1, source_target_pairs={{0,1},{1,0},{2,3},{3,2},{4,5},{5,4},{6,7},{7,6},{8,9},{9,8},{10,11... | collective-permute-start | bytes 786440 | tf_op jit(solution)/shard_map/ppermute | solution.py:332
  43.5 0.1 collective-permute-start.1
  43.7 1.4 collective-permute-start.2
  45.2 0.7 collective-permute-start.15
  45.9 3.5 %collective-permute-done.refs_1_ = bf16[1024,128]{1,0:T(8,128)(2,1)S(1)} collective-permute-done((bf16[1024,128]{1,0:T(8,128)(2,1)}, bf16[1024,128]{1,0:T(8,128)(2,1)S(1)}, u32[]{:S(2)}, u32[]{:S(2)}) %collective-permute-start) | collective-permute-done | bytes 262176 | tf_op jit(solution)/shard_map/ppermute | solution.py:332
  49.3 0.7 collective-permute-start.25
  50.0 1.3 collective-permute-start.14
  51.4 2.2 %shard_map.44 = (f32[8,512]{1,0:T(8,128)}, f32[8,512]{1,0:T(8,128)}, f32[8,512]{1,0:T(8,128)}) custom-call(s32[11]{0:T(128)} %stack.41.idx, f32[8,512]{1,0:T(8,128)} %copy-done.21, f32[8,512]{1,0:T(8,128)} %copy-done.22, f32[8,512]{1,0:T(8,128)} %copy-done.23, f32[8,512]{1,0:T(8,128)} %copy-done.24, f32[8,512]{1,0:T(8,128)} %get-tuple-element.33.refs_4_, ...), custom_call_target="tpu_custom_call" | custom-call | bytes 180224 | tf_op jit(solution)/shard_map/pallas_call | solution.py:301
  53.7 0.6 copy-done.15
  54.3 0.1 copy-done.16
  54.4 3.0 %shard_map.42 = (bf16[1024,128]{1,0:T(8,128)(2,1)}, bf16[1024,128]{1,0:T(8,128)(2,1)}, bf16[1024,128]{1,0:T(8,128)(2,1)}, bf16[1024,128]{1,0:T(8,128)(2,1)}) custom-call(s32[11]{0:T(128)} %stack.41.idx, bf16[1024,128]{1,0:T(8,128)(2,1)} %get-tuple-element.25.refs_0_, bf16[1024,128]{1,0:T(8,128)(2,1)} %copy-done.14, bf16[1024,128]{1,0:T(8,128)(2,1)} %copy-done.15, ...), custom_call_target="tpu_custom_call" | custom-call | bytes 2097152 | tf_op jit(solution)/shard_map/pallas_call | solution.py:301
  57.4 2.7 %collective-permute-start.6 = (bf16[1024,128]{1,0:T(8,128)(2,1)}, bf16[1024,128]{1,0:T(8,128)(2,1)S(1)}, u32[]{:S(2)}, u32[]{:S(2)}) collective-permute-start(bf16[1024,128]{1,0:T(8,128)(2,1)} %get-tuple-element.30), channel_id=1, source_target_pairs={{0,8},{1,9},{2,10},{3,11},{4,12},{5,13},{6,14},{7,15},{8,16},{9,17... | collective-permute-start | bytes 786440 | tf_op jit(solution)/shard_map/ppermute | solution.py:332
  60.1 8.6 %collective-permute-done.6.refs_0_ = bf16[1024,128]{1,0:T(8,128)(2,1)S(1)} collective-permute-done((bf16[1024,128]{1,0:T(8,128)(2,1)}, bf16[1024,128]{1,0:T(8,128)(2,1)S(1)}, u32[]{:S(2)}, u32[]{:S(2)}) %collective-permute-start.6) | collective-permute-done | bytes 262176 | tf_op jit(solution)/shard_map/ppermute | solution.py:332
  68.7 16.1 %collective-permute-done.7.refs_1_ = bf16[1024,128]{1,0:T(8,128)(2,1)S(1)} collective-permute-done((bf16[1024,128]{1,0:T(8,128)(2,1)}, bf16[1024,128]{1,0:T(8,128)(2,1)S(1)}, u32[]{:S(2)}, u32[]{:S(2)}) %collective-permute-start.7) | collective-permute-done | bytes 262176 | tf_op jit(solution)/shard_map/ppermute | solution.py:332
  84.8 2.2 %collective-permute-start.8 = (bf16[1024,128]{1,0:T(8,128)(2,1)}, bf16[1024,128]{1,0:T(8,128)(2,1)S(1)}, u32[]{:S(2)}, u32[]{:S(2)}) collective-permute-start(bf16[1024,128]{1,0:T(8,128)(2,1)} %get-tuple-element.32), channel_id=1, source_target_pairs={{0,24},{1,25},{2,26},{3,27},{4,28},{5,29},{6,30},{7,31},{8,0},{9,1... | collective-permute-start | bytes 786440 | tf_op jit(solution)/shard_map/ppermute | solution.py:332
  87.1 1.3 collective-permute-start.16
  88.4 1.5 collective-permute-start.26
  89.9 12.3 %shard_map.45 = (bf16[4,3,512,1024]{3,2,1,0:T(8,128)(2,1)}, bf16[4,1024,512]{2,1,0:T(8,128)(2,1)}, bf16[4,1024,1024]{2,1,0:T(8,128)(2,1)}, f32[4,1024,128]{2,1,0:T(8,128)}) custom-call(s32[11]{0:T(128)} %stack.41.idx, f32[8,512]{1,0:T(8,128)} %get-tuple-element.34.row_stat.refs_20_, f32[8,512]{1,0:T(8,128)} %get-tuple-element.35.own_stat.refs_21_, ...), custom_call_target="tpu_custom_call" | custom-call | flops 6442450944 | bytes 27328512 | tf_op jit(solution)/shard_map/pallas_call | solution.py:301
  102.2 0.7 copy-done.19
  103.0 3.5 %collective-permute-start.3 = (bf16[1024,128]{1,0:T(8,128)(2,1)S(1)}, bf16[1024,128]{1,0:T(8,128)(2,1)S(1)}, u32[]{:S(2)}, u32[]{:S(2)}) collective-permute-start(bf16[1024,128]{1,0:T(8,128)(2,1)S(1)} %copy-done.11), channel_id=1, source_target_pairs={{0,1},{1,0},{2,3},{3,2},{4,5},{5,4},{6,7},{7,6},{8,9},{9,8},{10,11... | collective-permute-start | bytes 786440 | tf_op jit(solution)/shard_map/ppermute | solution.py:332
  106.5 2.7 %shard_map.43.refs_4_ = bf16[3,1024,128]{2,1,0:T(8,128)(2,1)} custom-call(s32[11]{0:T(128)} %stack.41.idx, bf16[1024,128]{1,0:T(8,128)(2,1)} %copy-done.17, bf16[1024,128]{1,0:T(8,128)(2,1)} %copy-done.18, bf16[1024,128]{1,0:T(8,128)(2,1)} %copy-done.19), custom_call_target="tpu_custom_call" | custom-call | bytes 1572864 | tf_op jit(solution)/shard_map/pallas_call | solution.py:301
  109.2 1.5 collective-permute-start.5
  110.7 2.1 %collective-permute-done.26 = bf16[512,512]{1,0:T(8,128)(2,1)S(1)} collective-permute-done((bf16[512,512]{1,0:T(8,128)(2,1)S(1)}, bf16[512,512]{1,0:T(8,128)(2,1)S(1)}, u32[]{:S(2)}, u32[]{:S(2)}) %collective-permute-start.26) | collective-permute-done | bytes 524320 | tf_op jit(solution)/shard_map/ppermute | solution.py:332
  112.8 1.7 collective-permute-start.10
  114.5 12.3 %shard_map.46 = (bf16[4,3,512,1024]{3,2,1,0:T(8,128)(2,1)}, bf16[4,1024,512]{2,1,0:T(8,128)(2,1)}, bf16[4,1024,1024]{2,1,0:T(8,128)(2,1)}, f32[4,1024,128]{2,1,0:T(8,128)}) custom-call(s32[11]{0:T(128)} %stack.41.idx, f32[8,512]{1,0:T(8,128)} %get-tuple-element.34.row_stat.refs_20_, ...), custom_call_target="tpu_custom_call", output_to_operand_aliasing={{0}: (5, {}), {1}: (6, {}), {2}: (7, {}), {3}: (8, {})} | custom-call | flops 6442450944 | bytes 54591488 | tf_op jit(solution)/shard_map/pallas_call | solution.py:301
  126.8 0.1 add.22
  126.9 0.1 add.21
  127.0 0.3 add.20.refs_10_
  127.6 0.5 collective-permute-start.30
  128.0 0.1 collective-permute-start.29
  128.2 0.3 collective-permute-start.11
  128.5 22.8 %collective-permute-done.10.refs_6_ = bf16[3,1024,128]{2,1,0:T(8,128)(2,1)} collective-permute-done((bf16[3,1024,128]{2,1,0:T(8,128)(2,1)}, bf16[3,1024,128]{2,1,0:T(8,128)(2,1)}, u32[]{:S(2)}, u32[]{:S(2)}) %collective-permute-start.10) | collective-permute-done | bytes 786464 | tf_op jit(solution)/shard_map/ppermute | solution.py:332
  151.3 0.6 collective-permute-start.9
  151.8 15.2 %collective-permute-done.9.refs_5_ = bf16[3,1024,128]{2,1,0:T(8,128)(2,1)S(1)} collective-permute-done((bf16[3,1024,128]{2,1,0:T(8,128)(2,1)S(1)}, bf16[3,1024,128]{2,1,0:T(8,128)(2,1)S(1)}, u32[]{:S(2)}, u32[]{:S(2)}) %collective-permute-start.9) | collective-permute-done | bytes 786464 | tf_op jit(solution)/shard_map/ppermute | solution.py:332
  167.1 1.0 copy-done.7
  168.1 1.0 copy-done.8
  169.1 30.5 %shard_map.47 = (f32[1,512,2,512]{3,2,1,0:T(2,128)}, f32[1,512,2,512]{3,2,1,0:T(2,128)}) custom-call(s32[11]{0:T(128)} %stack.41.idx, bf16[1024,128]{1,0:T(8,128)(2,1)} %get-tuple-element.29.refs_0_, bf16[1024,128]{1,0:T(8,128)(2,1)} %copy-done.12, bf16[1024,128]{1,0:T(8,128)(2,1)} %copy-done.13, bf16[1024,128]{1,0:T(8,128)(2,1)} %collective-permute-done.5.refs_3_, ...), custom_call_target="tpu_custom_call" | custom-call | flops 8589934592 | bytes 44105728 | tf_op jit(solution)/shard_map/pallas_call | solution.py:301
  (83 shorter events, 0.5 us)
Async XLA Ops:
  0.6 43.0 %collective-permute-start.12 = (bf16[1024,512]{1,0:T(8,128)(2,1)}, bf16[1024,512]{1,0:T(8,128)(2,1)S(1)}, u32[]{:S(2)}, u32[]{:S(2)}) collective-permute-start(bf16[1024,512]{1,0:T(8,128)(2,1)} %refs_8_.1), channel_id=1, source_target_pairs={{0,8},{1,9},{2,10},{3,11},{4,12},{5,13},{6,14},{7,15},{8,0},{9,1},... | collective-permute-start | bytes 3145736 | tf_op jit(solution)/shard_map/ppermute | solution.py:332
  3.7 46.3 %collective-permute-start.13 = (bf16[1024,512]{1,0:T(8,128)(2,1)}, bf16[1024,512]{1,0:T(8,128)(2,1)S(1)}, u32[]{:S(2)}, u32[]{:S(2)}) collective-permute-start(bf16[1024,512]{1,0:T(8,128)(2,1)} %refs_8_.1), channel_id=1, source_target_pairs={{8,16},{9,17},{10,18},{11,19},{12,20},{13,21},{14,22},{15,23},{16,... | collective-permute-start | bytes 3145736 | tf_op jit(solution)/shard_map/ppermute | solution.py:332
  5.1 63.6 %copy-start.1 = (bf16[1024,512]{1,0:T(8,128)(2,1)S(1)}, bf16[1024,512]{1,0:T(8,128)(2,1)}, u32[]{:S(2)}) copy-start(bf16[1024,512]{1,0:T(8,128)(2,1)} %refs_8_.1) | copy-start | bytes 3145732
  8.4 11.1 %collective-permute-start.17 = (f32[8,512]{1,0:T(8,128)}, f32[8,512]{1,0:T(8,128)S(1)}, u32[]{:S(2)}, u32[]{:S(2)}) collective-permute-start(f32[8,512]{1,0:T(8,128)} %get-tuple-element.33.refs_4_), channel_id=1, source_target_pairs={{0,0},{1,8},{2,16},{3,24},{4,4},{5,12},{6,20},{7,28},{8,1},{9,9},{... | collective-permute-start | bytes 49160 | tf_op jit(solution)/shard_map/ppermute | solution.py:332
  9.8 22.8 %collective-permute-start.18 = (f32[8,512]{1,0:T(8,128)}, f32[8,512]{1,0:T(8,128)S(1)}, u32[]{:S(2)}, u32[]{:S(2)}) collective-permute-start(f32[8,512]{1,0:T(8,128)} %get-tuple-element.33.refs_4_), channel_id=1, source_target_pairs={{0,1},{1,9},{2,17},{3,25},{4,5},{5,13},{6,21},{7,29},{8,2},{9,10},... | collective-permute-start | bytes 49160 | tf_op jit(solution)/shard_map/ppermute | solution.py:332
  16.2 17.4 %collective-permute-start.19 = (f32[8,512]{1,0:T(8,128)}, f32[8,512]{1,0:T(8,128)S(1)}, u32[]{:S(2)}, u32[]{:S(2)}) collective-permute-start(f32[8,512]{1,0:T(8,128)} %get-tuple-element.33.refs_4_), channel_id=1, source_target_pairs={{0,2},{1,10},{2,18},{3,26},{4,6},{5,14},{6,22},{7,30},{8,3},{9,11}... | collective-permute-start | bytes 49160 | tf_op jit(solution)/shard_map/ppermute | solution.py:332
  19.5 31.8 %copy-start.21 = (f32[8,512]{1,0:T(8,128)}, f32[8,512]{1,0:T(8,128)S(1)}, u32[]{:S(2)}) copy-start(f32[8,512]{1,0:T(8,128)S(1)} %collective-permute-done.17.refs_0_) | copy-start | bytes 49156
  19.5 19.0 %collective-permute-start.20 = (f32[8,512]{1,0:T(8,128)}, f32[8,512]{1,0:T(8,128)S(1)}, u32[]{:S(2)}, u32[]{:S(2)}) collective-permute-start(f32[8,512]{1,0:T(8,128)} %get-tuple-element.33.refs_4_), channel_id=1, source_target_pairs={{0,3},{1,11},{2,19},{3,27},{4,7},{5,15},{6,23},{7,31},{8,0},{9,8},... | collective-permute-start | bytes 49160 | tf_op jit(solution)/shard_map/ppermute | solution.py:332
  32.6 18.8 %copy-start.22 = (f32[8,512]{1,0:T(8,128)}, f32[8,512]{1,0:T(8,128)S(1)}, u32[]{:S(2)}) copy-start(f32[8,512]{1,0:T(8,128)S(1)} %collective-permute-done.18.refs_1_) | copy-start | bytes 49156
  32.6 7.5 %collective-permute-start.21 = (f32[8,512]{1,0:T(8,128)}, f32[8,512]{1,0:T(8,128)S(1)}, u32[]{:S(2)}, u32[]{:S(2)}) collective-permute-start(f32[8,512]{1,0:T(8,128)} %get-tuple-element.33.refs_4_), channel_id=1, source_target_pairs={{0,8},{1,9},{2,10},{3,11},{4,12},{5,13},{6,14},{7,15},{8,16},{9,17... | collective-permute-start | bytes 49160 | tf_op jit(solution)/shard_map/ppermute | solution.py:332
  33.6 17.8 %copy-start.23 = (f32[8,512]{1,0:T(8,128)}, f32[8,512]{1,0:T(8,128)S(1)}, u32[]{:S(2)}) copy-start(f32[8,512]{1,0:T(8,128)S(1)} %collective-permute-done.19.refs_2_) | copy-start | bytes 49156
  33.6 9.9 %collective-permute-start.22 = (f32[8,512]{1,0:T(8,128)}, f32[8,512]{1,0:T(8,128)S(1)}, u32[]{:S(2)}, u32[]{:S(2)}) collective-permute-start(f32[8,512]{1,0:T(8,128)} %get-tuple-element.33.refs_4_), channel_id=1, source_target_pairs={{0,16},{1,17},{2,18},{3,19},{4,20},{5,21},{6,22},{7,23},{8,24},{9,... | collective-permute-start | bytes 49160 | tf_op jit(solution)/shard_map/ppermute | solution.py:332
  38.6 12.8 %copy-start.24 = (f32[8,512]{1,0:T(8,128)}, f32[8,512]{1,0:T(8,128)S(1)}, u32[]{:S(2)}) copy-start(f32[8,512]{1,0:T(8,128)S(1)} %collective-permute-done.20.refs_3_) | copy-start | bytes 49156
  38.6 6.6 %collective-permute-start.23 = (f32[8,512]{1,0:T(8,128)}, f32[8,512]{1,0:T(8,128)S(1)}, u32[]{:S(2)}, u32[]{:S(2)}) collective-permute-start(f32[8,512]{1,0:T(8,128)} %get-tuple-element.33.refs_4_), channel_id=1, source_target_pairs={{0,24},{1,25},{2,26},{3,27},{4,28},{5,29},{6,30},{7,31},{8,0},{9,1... | collective-permute-start | bytes 49160 | tf_op jit(solution)/shard_map/ppermute | solution.py:332
  40.1 11.3 %copy-start.25 = (f32[8,512]{1,0:T(8,128)}, f32[8,512]{1,0:T(8,128)S(1)}, u32[]{:S(2)}) copy-start(f32[8,512]{1,0:T(8,128)S(1)} %collective-permute-done.21.refs_5_) | copy-start | bytes 49156
  40.1 9.3 %collective-permute-start = (bf16[1024,128]{1,0:T(8,128)(2,1)}, bf16[1024,128]{1,0:T(8,128)(2,1)S(1)}, u32[]{:S(2)}, u32[]{:S(2)}) collective-permute-start(bf16[1024,128]{1,0:T(8,128)(2,1)} %get-tuple-element.26), channel_id=1, source_target_pairs={{0,1},{1,0},{2,3},{3,2},{4,5},{5,4},{6,7},{7,6},{8,9},{9,8},{10,11... | collective-permute-start | bytes 786440 | tf_op jit(solution)/shard_map/ppermute | solution.py:332
  43.5 7.9 %copy-start.26 = (f32[8,512]{1,0:T(8,128)}, f32[8,512]{1,0:T(8,128)S(1)}, u32[]{:S(2)}) copy-start(f32[8,512]{1,0:T(8,128)S(1)} %collective-permute-done.22.refs_6_) | copy-start | bytes 49156
  43.5 10.0 %collective-permute-start.1 = (bf16[1024,128]{1,0:T(8,128)(2,1)}, bf16[1024,128]{1,0:T(8,128)(2,1)S(1)}, u32[]{:S(2)}, u32[]{:S(2)}) collective-permute-start(bf16[1024,128]{1,0:T(8,128)(2,1)} %get-tuple-element.27), channel_id=1, source_target_pairs={{0,2},{1,3},{2,0},{3,1},{4,6},{5,7},{6,4},{7,5},{8,10},{9,11},{10,... | collective-permute-start | bytes 786440 | tf_op jit(solution)/shard_map/ppermute | solution.py:332
  43.7 83.8 %copy-start.2 = (bf16[1024,512]{1,0:T(8,128)(2,1)}, bf16[1024,512]{1,0:T(8,128)(2,1)S(1)}, u32[]{:S(2)}) copy-start(bf16[1024,512]{1,0:T(8,128)(2,1)S(1)} %collective-permute-done.12.refs_9_) | copy-start | bytes 3145732
  43.7 10.0 %collective-permute-start.2 = (bf16[1024,128]{1,0:T(8,128)(2,1)}, bf16[1024,128]{1,0:T(8,128)(2,1)S(1)}, u32[]{:S(2)}, u32[]{:S(2)}) collective-permute-start(bf16[1024,128]{1,0:T(8,128)(2,1)} %get-tuple-element.28), channel_id=1, source_target_pairs={{0,3},{1,2},{2,1},{3,0},{4,7},{5,6},{6,5},{7,4},{8,11},{9,10},{10,... | collective-permute-start | bytes 786440 | tf_op jit(solution)/shard_map/ppermute | solution.py:332
  45.2 41.9 %collective-permute-start.15 = (bf16[512,512]{1,0:T(8,128)(2,1)S(1)}, bf16[512,512]{1,0:T(8,128)(2,1)S(1)}, u32[]{:S(2)}, u32[]{:S(2)}) collective-permute-start(bf16[512,512]{1,0:T(8,128)(2,1)S(1)} %get-tuple-element.49), channel_id=1, source_target_pairs={{8,16},{9,17},{10,18},{11,19},{12,20},{13,21},{14,22},{15,23},{16,... | collective-permute-start | bytes 1572872 | tf_op jit(solution)/shard_map/ppermute | solution.py:332
  49.3 39.0 %collective-permute-start.25 = (bf16[512,512]{1,0:T(8,128)(2,1)S(1)}, bf16[512,512]{1,0:T(8,128)(2,1)S(1)}, u32[]{:S(2)}, u32[]{:S(2)}) collective-permute-start(bf16[512,512]{1,0:T(8,128)(2,1)S(1)} %get-tuple-element.48), channel_id=1, source_target_pairs={{8,16},{9,17},{10,18},{11,19},{12,20},{13,21},{14,22},{15,23},{16,... | collective-permute-start | bytes 1572872 | tf_op jit(solution)/shard_map/ppermute | solution.py:332
  50.0 59.2 %collective-permute-start.14 = (bf16[1024,512]{1,0:T(8,128)(2,1)S(1)}, bf16[1024,512]{1,0:T(8,128)(2,1)S(1)}, u32[]{:S(2)}, u32[]{:S(2)}) collective-permute-start(bf16[1024,512]{1,0:T(8,128)(2,1)S(1)} %collective-permute-done.13), channel_id=1, source_target_pairs={{8,0},{9,1},{10,2},{11,3},{12,4},{13,5},{14,6},{15,7},{16,24},{17,... | collective-permute-start | bytes 3145736 | tf_op jit(solution)/shard_map/ppermute | solution.py:332
  53.6 6.5 %collective-permute-start.24 = (f32[8,512]{1,0:T(8,128)}, f32[8,512]{1,0:T(8,128)S(1)}, u32[]{:S(2)}, u32[]{:S(2)}) collective-permute-start(f32[8,512]{1,0:T(8,128)} %get-tuple-element.35.own_stat.refs_21_), channel_id=1, source_target_pairs={{0,4},{1,5},{2,6},{3,7},{4,0},{5,1},{6,2},{7,3},{8,12},{9,13},{10,... | collective-permute-start | bytes 49160 | tf_op jit(solution)/shard_map/ppermute | solution.py:332
  57.4 11.3 %collective-permute-start.6 = (bf16[1024,128]{1,0:T(8,128)(2,1)}, bf16[1024,128]{1,0:T(8,128)(2,1)S(1)}, u32[]{:S(2)}, u32[]{:S(2)}) collective-permute-start(bf16[1024,128]{1,0:T(8,128)(2,1)} %get-tuple-element.30), channel_id=1, source_target_pairs={{0,8},{1,9},{2,10},{3,11},{4,12},{5,13},{6,14},{7,15},{8,16},{9,17... | collective-permute-start | bytes 786440 | tf_op jit(solution)/shard_map/ppermute | solution.py:332
  60.1 29.7 %copy-start.20 = (f32[8,512]{1,0:T(8,128)}, f32[8,512]{1,0:T(8,128)S(1)}, u32[]{:S(2)}) copy-start(f32[8,512]{1,0:T(8,128)S(1)} %collective-permute-done.24.mate_stat.refs_22_) | copy-start | bytes 49156
  60.1 24.7 %collective-permute-start.7 = (bf16[1024,128]{1,0:T(8,128)(2,1)}, bf16[1024,128]{1,0:T(8,128)(2,1)S(1)}, u32[]{:S(2)}, u32[]{:S(2)}) collective-permute-start(bf16[1024,128]{1,0:T(8,128)(2,1)} %get-tuple-element.31), channel_id=1, source_target_pairs={{0,16},{1,17},{2,18},{3,19},{4,20},{5,21},{6,22},{7,23},{8,24},{9,... | collective-permute-start | bytes 786440 | tf_op jit(solution)/shard_map/ppermute | solution.py:332
  68.7 33.5 %copy-start.17 = (bf16[1024,128]{1,0:T(8,128)(2,1)}, bf16[1024,128]{1,0:T(8,128)(2,1)S(1)}, u32[]{:S(2)}) copy-start(bf16[1024,128]{1,0:T(8,128)(2,1)S(1)} %collective-permute-done.6.refs_0_) | copy-start | bytes 786436
  68.7 59.4 %collective-permute-start.27 = (bf16[1024,512]{1,0:T(8,128)(2,1)S(1)}, bf16[1024,512]{1,0:T(8,128)(2,1)S(1)}, u32[]{:S(2)}, u32[]{:S(2)}) collective-permute-start(bf16[1024,512]{1,0:T(8,128)(2,1)S(1)} %copy-done.1), channel_id=1, source_target_pairs={{0,4},{1,5},{2,6},{3,7},{4,0},{5,1},{6,2},{7,3},{8,12},{9,13},{10,... | collective-permute-start | bytes 3145736 | tf_op jit(solution)/shard_map/ppermute | solution.py:332
  84.8 17.4 %collective-permute-start.8 = (bf16[1024,128]{1,0:T(8,128)(2,1)}, bf16[1024,128]{1,0:T(8,128)(2,1)S(1)}, u32[]{:S(2)}, u32[]{:S(2)}) collective-permute-start(bf16[1024,128]{1,0:T(8,128)(2,1)} %get-tuple-element.32), channel_id=1, source_target_pairs={{0,24},{1,25},{2,26},{3,27},{4,28},{5,29},{6,30},{7,31},{8,0},{9,1... | collective-permute-start | bytes 786440 | tf_op jit(solution)/shard_map/ppermute | solution.py:332
  87.1 22.1 %collective-permute-start.16 = (bf16[512,512]{1,0:T(8,128)(2,1)S(1)}, bf16[512,512]{1,0:T(8,128)(2,1)S(1)}, u32[]{:S(2)}, u32[]{:S(2)}) collective-permute-start(bf16[512,512]{1,0:T(8,128)(2,1)S(1)} %collective-permute-done.15), channel_id=1, source_target_pairs={{8,0},{9,1},{10,2},{11,3},{12,4},{13,5},{14,6},{15,7},{16,24},{17,... | collective-permute-start | bytes 1572872 | tf_op jit(solution)/shard_map/ppermute | solution.py:332
  88.4 24.4 %collective-permute-start.26 = (bf16[512,512]{1,0:T(8,128)(2,1)S(1)}, bf16[512,512]{1,0:T(8,128)(2,1)S(1)}, u32[]{:S(2)}, u32[]{:S(2)}) collective-permute-start(bf16[512,512]{1,0:T(8,128)(2,1)S(1)} %collective-permute-done.25), channel_id=1, source_target_pairs={{8,0},{9,1},{10,2},{11,3},{12,4},{13,5},{14,6},{15,7},{16,24},{17,... | collective-permute-start | bytes 1572872 | tf_op jit(solution)/shard_map/ppermute | solution.py:332
  89.9 13.1 %copy-start.11 = (bf16[1024,128]{1,0:T(8,128)(2,1)S(1)}, bf16[1024,128]{1,0:T(8,128)(2,1)}, u32[]{:S(2)}) copy-start(bf16[1024,128]{1,0:T(8,128)(2,1)} %get-tuple-element.29.refs_0_) | copy-start | bytes 786436
  103.0 24.5 %collective-permute-start.3 = (bf16[1024,128]{1,0:T(8,128)(2,1)S(1)}, bf16[1024,128]{1,0:T(8,128)(2,1)S(1)}, u32[]{:S(2)}, u32[]{:S(2)}) collective-permute-start(bf16[1024,128]{1,0:T(8,128)(2,1)S(1)} %copy-done.11), channel_id=1, source_target_pairs={{0,1},{1,0},{2,3},{3,2},{4,5},{5,4},{6,7},{7,6},{8,9},{9,8},{10,11... | collective-permute-start | bytes 786440 | tf_op jit(solution)/shard_map/ppermute | solution.py:332
  109.2 18.3 %collective-permute-start.4 = (bf16[1024,128]{1,0:T(8,128)(2,1)S(1)}, bf16[1024,128]{1,0:T(8,128)(2,1)S(1)}, u32[]{:S(2)}, u32[]{:S(2)}) collective-permute-start(bf16[1024,128]{1,0:T(8,128)(2,1)S(1)} %copy-done.11), channel_id=1, source_target_pairs={{0,2},{1,3},{2,0},{3,1},{4,6},{5,7},{6,4},{7,5},{8,10},{9,11},{10,... | collective-permute-start | bytes 786440 | tf_op jit(solution)/shard_map/ppermute | solution.py:332
  109.2 18.8 %collective-permute-start.5 = (bf16[1024,128]{1,0:T(8,128)(2,1)S(1)}, bf16[1024,128]{1,0:T(8,128)(2,1)}, u32[]{:S(2)}, u32[]{:S(2)}) collective-permute-start(bf16[1024,128]{1,0:T(8,128)(2,1)S(1)} %copy-done.11), channel_id=1, source_target_pairs={{0,3},{1,2},{2,1},{3,0},{4,7},{5,6},{6,5},{7,4},{8,11},{9,10},{10,... | collective-permute-start | bytes 786440 | tf_op jit(solution)/shard_map/ppermute | solution.py:332
  112.8 38.5 %collective-permute-start.10 = (bf16[3,1024,128]{2,1,0:T(8,128)(2,1)}, bf16[3,1024,128]{2,1,0:T(8,128)(2,1)}, u32[]{:S(2)}, u32[]{:S(2)}) collective-permute-start(bf16[3,1024,128]{2,1,0:T(8,128)(2,1)} %shard_map.43.refs_4_), channel_id=1, source_target_pairs={{0,2},{1,3},{2,0},{3,1},{4,6},{5,7},{6,4},{7,5},{8,10},{9,11},{10,... | collective-permute-start | bytes 2359304 | tf_op jit(solution)/shard_map/ppermute | solution.py:332
  127.3 41.8 %copy-start = (bf16[1024,512]{1,0:T(8,128)(2,1)}, bf16[1024,512]{1,0:T(8,128)(2,1)S(1)}, u32[]{:S(2)}) copy-start(bf16[1024,512]{1,0:T(8,128)(2,1)S(1)} %add.20.refs_10_) | copy-start | bytes 3145732
  127.4 41.7 %copy-start.3 = (bf16[1024,512]{1,0:T(8,128)(2,1)}, bf16[1024,512]{1,0:T(8,128)(2,1)S(1)}, u32[]{:S(2)}) copy-start(bf16[1024,512]{1,0:T(8,128)(2,1)S(1)} %pad_maximum_fusion.refs_11_) | copy-start | bytes 3145732
  127.5 41.6 %copy-start.12 = (bf16[1024,128]{1,0:T(8,128)(2,1)}, bf16[1024,128]{1,0:T(8,128)(2,1)S(1)}, u32[]{:S(2)}) copy-start(bf16[1024,128]{1,0:T(8,128)(2,1)S(1)} %collective-permute-done.3.refs_1_) | copy-start | bytes 786436
  127.5 39.6 %collective-permute-start.28 = (bf16[1024,512]{1,0:T(8,128)(2,1)S(1)}, bf16[1024,512]{1,0:T(8,128)(2,1)S(1)}, u32[]{:S(2)}, u32[]{:S(2)}) collective-permute-start(bf16[1024,512]{1,0:T(8,128)(2,1)S(1)} %collective-permute-done.12.refs_9_), channel_id=1, source_target_pairs={{0,4},{1,5},{2,6},{3,7},{4,0},{5,1},{6,2},{7,3},{8,12},{9,13},{10,... | collective-permute-start | bytes 3145736 | tf_op jit(solution)/shard_map/ppermute | solution.py:332
  127.6 41.5 %copy-start.13 = (bf16[1024,128]{1,0:T(8,128)(2,1)}, bf16[1024,128]{1,0:T(8,128)(2,1)S(1)}, u32[]{:S(2)}) copy-start(bf16[1024,128]{1,0:T(8,128)(2,1)S(1)} %collective-permute-done.4.refs_2_) | copy-start | bytes 786436
  127.6 39.5 %collective-permute-start.30 = (bf16[1024,512]{1,0:T(8,128)(2,1)S(1)}, bf16[1024,512]{1,0:T(8,128)(2,1)S(1)}, u32[]{:S(2)}, u32[]{:S(2)}) collective-permute-start(bf16[1024,512]{1,0:T(8,128)(2,1)S(1)} %pad_maximum_fusion.refs_11_), channel_id=1, source_target_pairs={{0,4},{1,5},{2,6},{3,7},{4,0},{5,1},{6,2},{7,3},{8,12},{9,13},{10,... | collective-permute-start | bytes 3145736 | tf_op jit(solution)/shard_map/ppermute | solution.py:332
  128.0 39.0 %collective-permute-start.29 = (bf16[1024,512]{1,0:T(8,128)(2,1)S(1)}, bf16[1024,512]{1,0:T(8,128)(2,1)S(1)}, u32[]{:S(2)}, u32[]{:S(2)}) collective-permute-start(bf16[1024,512]{1,0:T(8,128)(2,1)S(1)} %add.20.refs_10_), channel_id=1, source_target_pairs={{0,4},{1,5},{2,6},{3,7},{4,0},{5,1},{6,2},{7,3},{8,12},{9,13},{10,... | collective-permute-start | bytes 3145736 | tf_op jit(solution)/shard_map/ppermute | solution.py:332
  128.2 40.9 %copy-start.5 = (bf16[1024,512]{1,0:T(8,128)(2,1)}, bf16[1024,512]{1,0:T(8,128)(2,1)S(1)}, u32[]{:S(2)}) copy-start(bf16[1024,512]{1,0:T(8,128)(2,1)S(1)} %collective-permute-done.27.refs_12_) | copy-start | bytes 3145732
  128.2 23.7 %collective-permute-start.11 = (bf16[3,1024,128]{2,1,0:T(8,128)(2,1)S(1)}, bf16[3,1024,128]{2,1,0:T(8,128)(2,1)S(1)}, u32[]{:S(2)}, u32[]{:S(2)}) collective-permute-start(bf16[3,1024,128]{2,1,0:T(8,128)(2,1)S(1)} %copy-done.4), channel_id=1, source_target_pairs={{0,3},{1,2},{2,1},{3,0},{4,7},{5,6},{6,5},{7,4},{8,11},{9,10},{10,... | collective-permute-start | bytes 2359304 | tf_op jit(solution)/shard_map/ppermute | solution.py:332
  151.3 15.8 %collective-permute-start.9 = (bf16[3,1024,128]{2,1,0:T(8,128)(2,1)S(1)}, bf16[3,1024,128]{2,1,0:T(8,128)(2,1)S(1)}, u32[]{:S(2)}, u32[]{:S(2)}) collective-permute-start(bf16[3,1024,128]{2,1,0:T(8,128)(2,1)S(1)} %copy-done.4), channel_id=1, source_target_pairs={{0,1},{1,0},{2,3},{3,2},{4,5},{5,4},{6,7},{7,6},{8,9},{9,8},{10,11... | collective-permute-start | bytes 2359304 | tf_op jit(solution)/shard_map/ppermute | solution.py:332
  151.8 17.3 %copy-start.9 = (bf16[3,1024,128]{2,1,0:T(8,128)(2,1)}, bf16[3,1024,128]{2,1,0:T(8,128)(2,1)S(1)}, u32[]{:S(2)}) copy-start(bf16[3,1024,128]{2,1,0:T(8,128)(2,1)S(1)} %collective-permute-done.11.refs_7_) | copy-start | bytes 2359300
  (11 other events, 25.1 us)

commit v3 on v2

--- a/solution.py
+++ b/solution.py
@@ -202,8 +202,9 @@
     urow_hbm, ucol_hbm, inv_hbm, w_hbm, row_stat, own_stat, mate_stat, ld_ref, rg_ref, se_ref = refs[:10]
     rows_v, own_v, mate_v, urow_v, ucol_v, inv_v, zu_v, zinv_v, zcol_v, y_v, w_v, rs_v, cs_v, sems, w_sem = refs[10:]
     piece = first[0].shape[1]
-    tile, width = rg_ref.shape[1], rg_ref.shape[3]
-    snps = own[0].shape[0]
+    snps, width = own[0].shape
+    stride = 2 * width // lanes
+    tile = rg_ref.shape[0] // stride
     side = idx[1]
     step_id = pl.program_id(0)
     w_copy = pltpu.make_async_copy(w_hbm, w_v, w_sem.at[0])
@@ -277,7 +278,7 @@
         for group in range(2 * width // lanes):
             at = slice(group * lanes, (group + 1) * lanes)
             half, inner = divmod(group * lanes, width)
-            place = slice(inner, inner + lanes)
+            place = pl.ds(inner // lanes * 2 + half, tile, stride=stride)
             t = [[y_v[s, k, here, at].astype(f32) for s in range(blocks)] for k in range(2)]
             t += [[w_v[s, k, here, at].astype(f32) for s in range(blocks)] for k in range(3)]
             sums = [sum(x[1:], x[0]) for x in t]
@@ -285,11 +286,11 @@
             for s in range(blocks + 1):
                 tiles = sums if s == 0 else [total_ - x[s - 1] for total_, x in zip(sums, t)]
                 values.append(coupling(tiles) * (rs_v[s, here, :] * cs_v[s : s + 1, at]))
-            rg_ref[0, :, half, place] = values[0]
+            rg_ref[place, :] = values[0]
             dels = values[1:]
             mean = sum(dels[1:], dels[0]) * (1.0 / blocks)
             spread = sum([(d - mean) * (d - mean) for d in dels[1:]], (dels[0] - mean) * (dels[0] - mean))
-            se_ref[0, :, half, place] = jnp.sqrt((blocks - 1) / blocks * spread)
+            se_ref[place, :] = jnp.sqrt((blocks - 1) / blocks * spread)
 
 
 def whole(shape):
@@ -435,11 +436,13 @@
     own = [zscores, near, inner + outer]
     own.append(jnp.concatenate([cross[k] + last[k] for k in range(2)], axis=0))
     mate = mate + [swap(own[slot]) for slot in (2, 3)]
-    small = tile // 2
-    out = jax.ShapeDtypeStruct((1, width, grid_rows, width), f32)
-    out_spec = pl.BlockSpec((1, small, grid_rows, width), lambda i, _: (0, jnp.maximum(i - 1, 0), 0, 0))
+    small = tile
+    groups = width // lanes
+    out = jax.ShapeDtypeStruct((width * groups * grid_rows, lanes), f32)
+    out_spec = pl.BlockSpec((small * groups * grid_rows, lanes), lambda i, _: (jnp.maximum(i - 1, 0), 0))
     return tuple(
-        call(
+        flat.reshape(width, groups, grid_rows, lanes).transpose(0, 2, 1, 3).reshape(1, width, grid_rows, width)
+        for flat in call(
             functools.partial(finish_kernel, parts, blocks),
             idx,
             (*first, *rows, *own, *mate, u_row, u_col, inv_col, w_sums, *stats),

time: 201 us -> 199 us (0.990)
  Pallas kernels: 66.3 us -> 64.2 us
    pallas_call x7, Pallas kernels: 66.3 us -> 64.2 us  [call(): pl.pallas_call(kernel, input_output_aliases=aliases, grid_spec=pltpu.Pref...]
where the time goes in v3:
time: 199 us; the launch traced here: 198 us
  waiting for transfers between devices  69.4 us (35%)
  Pallas kernels  64.2 us (32%)
  starting transfers between devices  58.1 us (29%)
  local copies, waits for them, and re-layouts  4.15 us (2%)
    ppermute x31, waiting for transfers between devices, move(): return lax.ppermute(value, axes, pairs)  69.4 us
    pallas_call x7, Pallas kernels, call(): pl.pallas_call(kernel, input_output_aliases=aliases, grid_spec=pltpu.Pref...  64.2 us
    ppermute x31, starting transfers between devices, move(): return lax.ppermute(value, axes, pairs)  58.1 us
  transfers between devices with their start and end apart: 31, of which 7 were waited for; matrix products, arithmetic and copies ran while one was open for 1% of the time, Pallas kernels for 18%

profile of v3, /device:TPU:0, one launch (start us, length us, event | category | flops | bytes accessed | tf_op | source)
XLA Modules:
  0.0 197.7 jit_solution(16993342887800538104)
XLA Ops:
  0.6 3.1 %collective-permute-start.12 = (bf16[1024,512]{1,0:T(8,128)(2,1)}, bf16[1024,512]{1,0:T(8,128)(2,1)S(1)}, u32[]{:S(2)}, u32[]{:S(2)}) collective-permute-start(bf16[1024,512]{1,0:T(8,128)(2,1)} %refs_8_.1), channel_id=1, source_target_pairs={{0,8},{1,9},{2,10},{3,11},{4,12},{5,13},{6,14},{7,15},{8,0},{9,1},... | collective-permute-start | bytes 3145736 | tf_op jit(solution)/shard_map/ppermute | solution.py:333
  3.7 0.7 collective-permute-start.13
  4.5 0.6 stack.41.idx
  5.1 3.3 %shard_map.41 = (f32[8,512]{1,0:T(8,128)}, bf16[1024,128]{1,0:T(8,128)(2,1)}, bf16[1024,128]{1,0:T(8,128)(2,1)}, bf16[1024,128]{1,0:T(8,128)(2,1)}, bf16[1024,128]{1,0:T(8,128)(2,1)}) custom-call(s32[11]{0:T(128)} %stack.41.idx, bf16[1024,512]{1,0:T(8,128)(2,1)} %refs_8_.1, f32[8,128]{1,0:T(8,128)} %bitcast.20), custom_call_target="tpu_custom_call" | custom-call | bytes 2117632 | tf_op jit(solution)/shard_map/pallas_call | solution.py:302
  8.4 1.4 collective-permute-start.17
  9.8 6.4 %collective-permute-start.18 = (f32[8,512]{1,0:T(8,128)}, f32[8,512]{1,0:T(8,128)S(1)}, u32[]{:S(2)}, u32[]{:S(2)}) collective-permute-start(f32[8,512]{1,0:T(8,128)} %get-tuple-element.35.refs_4_), channel_id=1, source_target_pairs={{0,1},{1,9},{2,17},{3,25},{4,5},{5,13},{6,21},{7,29},{8,2},{9,10},... | collective-permute-start | bytes 49160 | tf_op jit(solution)/shard_map/ppermute | solution.py:333
  16.2 3.3 %collective-permute-start.19 = (f32[8,512]{1,0:T(8,128)}, f32[8,512]{1,0:T(8,128)S(1)}, u32[]{:S(2)}, u32[]{:S(2)}) collective-permute-start(f32[8,512]{1,0:T(8,128)} %get-tuple-element.35.refs_4_), channel_id=1, source_target_pairs={{0,2},{1,10},{2,18},{3,26},{4,6},{5,14},{6,22},{7,30},{8,3},{9,11}... | collective-permute-start | bytes 49160 | tf_op jit(solution)/shard_map/ppermute | solution.py:333
  19.5 13.1 %collective-permute-start.20 = (f32[8,512]{1,0:T(8,128)}, f32[8,512]{1,0:T(8,128)S(1)}, u32[]{:S(2)}, u32[]{:S(2)}) collective-permute-start(f32[8,512]{1,0:T(8,128)} %get-tuple-element.35.refs_4_), channel_id=1, source_target_pairs={{0,3},{1,11},{2,19},{3,27},{4,7},{5,15},{6,23},{7,31},{8,0},{9,8},... | collective-permute-start | bytes 49160 | tf_op jit(solution)/shard_map/ppermute | solution.py:333
  32.6 1.0 collective-permute-done.19.refs_2_
  33.6 4.9 %collective-permute-start.22 = (f32[8,512]{1,0:T(8,128)}, f32[8,512]{1,0:T(8,128)S(1)}, u32[]{:S(2)}, u32[]{:S(2)}) collective-permute-start(f32[8,512]{1,0:T(8,128)} %get-tuple-element.35.refs_4_), channel_id=1, source_target_pairs={{0,16},{1,17},{2,18},{3,19},{4,20},{5,21},{6,22},{7,23},{8,24},{9,... | collective-permute-start | bytes 49160 | tf_op jit(solution)/shard_map/ppermute | solution.py:333
  38.6 1.5 collective-permute-start.23
  40.1 3.5 %collective-permute-start = (bf16[1024,128]{1,0:T(8,128)(2,1)}, bf16[1024,128]{1,0:T(8,128)(2,1)S(1)}, u32[]{:S(2)}, u32[]{:S(2)}) collective-permute-start(bf16[1024,128]{1,0:T(8,128)(2,1)} %get-tuple-element.28), channel_id=1, source_target_pairs={{0,1},{1,0},{2,3},{3,2},{4,5},{5,4},{6,7},{7,6},{8,9},{9,8},{10,11... | collective-permute-start | bytes 786440 | tf_op jit(solution)/shard_map/ppermute | solution.py:333
  43.5 0.1 collective-permute-start.1
  43.7 1.4 collective-permute-start.2
  45.2 0.7 collective-permute-start.15
  45.9 3.5 %collective-permute-done.refs_1_ = bf16[1024,128]{1,0:T(8,128)(2,1)S(1)} collective-permute-done((bf16[1024,128]{1,0:T(8,128)(2,1)}, bf16[1024,128]{1,0:T(8,128)(2,1)S(1)}, u32[]{:S(2)}, u32[]{:S(2)}) %collective-permute-start) | collective-permute-done | bytes 262176 | tf_op jit(solution)/shard_map/ppermute | solution.py:333
  49.3 0.7 collective-permute-start.25
  50.0 1.3 collective-permute-start.14
  51.4 2.2 %shard_map.44 = (f32[8,512]{1,0:T(8,128)}, f32[8,512]{1,0:T(8,128)}, f32[8,512]{1,0:T(8,128)}) custom-call(s32[11]{0:T(128)} %stack.41.idx, f32[8,512]{1,0:T(8,128)} %copy-done.21, f32[8,512]{1,0:T(8,128)} %copy-done.22, f32[8,512]{1,0:T(8,128)} %copy-done.23, f32[8,512]{1,0:T(8,128)} %copy-done.24, f32[8,512]{1,0:T(8,128)} %get-tuple-element.35.refs_4_, ...), custom_call_target="tpu_custom_call" | custom-call | bytes 180224 | tf_op jit(solution)/shard_map/pallas_call | solution.py:302
  53.7 0.6 copy-done.15
  54.3 0.1 copy-done.16
  54.4 3.0 %shard_map.42 = (bf16[1024,128]{1,0:T(8,128)(2,1)}, bf16[1024,128]{1,0:T(8,128)(2,1)}, bf16[1024,128]{1,0:T(8,128)(2,1)}, bf16[1024,128]{1,0:T(8,128)(2,1)}) custom-call(s32[11]{0:T(128)} %stack.41.idx, bf16[1024,128]{1,0:T(8,128)(2,1)} %get-tuple-element.27.refs_0_, bf16[1024,128]{1,0:T(8,128)(2,1)} %copy-done.14, bf16[1024,128]{1,0:T(8,128)(2,1)} %copy-done.15, ...), custom_call_target="tpu_custom_call" | custom-call | bytes 2097152 | tf_op jit(solution)/shard_map/pallas_call | solution.py:302
  57.4 2.7 %collective-permute-start.6 = (bf16[1024,128]{1,0:T(8,128)(2,1)}, bf16[1024,128]{1,0:T(8,128)(2,1)S(1)}, u32[]{:S(2)}, u32[]{:S(2)}) collective-permute-start(bf16[1024,128]{1,0:T(8,128)(2,1)} %get-tuple-element.32), channel_id=1, source_target_pairs={{0,8},{1,9},{2,10},{3,11},{4,12},{5,13},{6,14},{7,15},{8,16},{9,17... | collective-permute-start | bytes 786440 | tf_op jit(solution)/shard_map/ppermute | solution.py:333
  60.1 8.6 %collective-permute-done.6.refs_0_ = bf16[1024,128]{1,0:T(8,128)(2,1)S(1)} collective-permute-done((bf16[1024,128]{1,0:T(8,128)(2,1)}, bf16[1024,128]{1,0:T(8,128)(2,1)S(1)}, u32[]{:S(2)}, u32[]{:S(2)}) %collective-permute-start.6) | collective-permute-done | bytes 262176 | tf_op jit(solution)/shard_map/ppermute | solution.py:333
  68.7 16.1 %collective-permute-done.7.refs_1_ = bf16[1024,128]{1,0:T(8,128)(2,1)S(1)} collective-permute-done((bf16[1024,128]{1,0:T(8,128)(2,1)}, bf16[1024,128]{1,0:T(8,128)(2,1)S(1)}, u32[]{:S(2)}, u32[]{:S(2)}) %collective-permute-start.7) | collective-permute-done | bytes 262176 | tf_op jit(solution)/shard_map/ppermute | solution.py:333
  84.8 2.2 %collective-permute-start.8 = (bf16[1024,128]{1,0:T(8,128)(2,1)}, bf16[1024,128]{1,0:T(8,128)(2,1)S(1)}, u32[]{:S(2)}, u32[]{:S(2)}) collective-permute-start(bf16[1024,128]{1,0:T(8,128)(2,1)} %get-tuple-element.34), channel_id=1, source_target_pairs={{0,24},{1,25},{2,26},{3,27},{4,28},{5,29},{6,30},{7,31},{8,0},{9,1... | collective-permute-start | bytes 786440 | tf_op jit(solution)/shard_map/ppermute | solution.py:333
  87.1 1.3 collective-permute-start.16
  88.4 1.5 collective-permute-start.26
  89.9 12.4 %shard_map.45 = (bf16[4,3,512,1024]{3,2,1,0:T(8,128)(2,1)}, bf16[4,1024,512]{2,1,0:T(8,128)(2,1)}, bf16[4,1024,1024]{2,1,0:T(8,128)(2,1)}, f32[4,1024,128]{2,1,0:T(8,128)}) custom-call(s32[11]{0:T(128)} %stack.41.idx, f32[8,512]{1,0:T(8,128)} %get-tuple-element.36.row_stat.refs_20_, f32[8,512]{1,0:T(8,128)} %get-tuple-element.37.own_stat.refs_21_, ...), custom_call_target="tpu_custom_call" | custom-call | flops 6442450944 | bytes 27328512 | tf_op jit(solution)/shard_map/pallas_call | solution.py:302
  102.3 0.7 copy-done.19
  103.0 3.5 %collective-permute-start.3 = (bf16[1024,128]{1,0:T(8,128)(2,1)S(1)}, bf16[1024,128]{1,0:T(8,128)(2,1)S(1)}, u32[]{:S(2)}, u32[]{:S(2)}) collective-permute-start(bf16[1024,128]{1,0:T(8,128)(2,1)S(1)} %copy-done.11), channel_id=1, source_target_pairs={{0,1},{1,0},{2,3},{3,2},{4,5},{5,4},{6,7},{7,6},{8,9},{9,8},{10,11... | collective-permute-start | bytes 786440 | tf_op jit(solution)/shard_map/ppermute | solution.py:333
  106.5 2.7 %shard_map.43.refs_4_ = bf16[3,1024,128]{2,1,0:T(8,128)(2,1)} custom-call(s32[11]{0:T(128)} %stack.41.idx, bf16[1024,128]{1,0:T(8,128)(2,1)} %copy-done.17, bf16[1024,128]{1,0:T(8,128)(2,1)} %copy-done.18, bf16[1024,128]{1,0:T(8,128)(2,1)} %copy-done.19), custom_call_target="tpu_custom_call" | custom-call | bytes 1572864 | tf_op jit(solution)/shard_map/pallas_call | solution.py:302
  109.2 1.5 collective-permute-start.5
  110.7 2.1 %collective-permute-done.26 = bf16[512,512]{1,0:T(8,128)(2,1)S(1)} collective-permute-done((bf16[512,512]{1,0:T(8,128)(2,1)S(1)}, bf16[512,512]{1,0:T(8,128)(2,1)S(1)}, u32[]{:S(2)}, u32[]{:S(2)}) %collective-permute-start.26) | collective-permute-done | bytes 524320 | tf_op jit(solution)/shard_map/ppermute | solution.py:333
  112.8 1.7 collective-permute-start.10
  114.5 12.3 %shard_map.46 = (bf16[4,3,512,1024]{3,2,1,0:T(8,128)(2,1)}, bf16[4,1024,512]{2,1,0:T(8,128)(2,1)}, bf16[4,1024,1024]{2,1,0:T(8,128)(2,1)}, f32[4,1024,128]{2,1,0:T(8,128)}) custom-call(s32[11]{0:T(128)} %stack.41.idx, f32[8,512]{1,0:T(8,128)} %get-tuple-element.36.row_stat.refs_20_, ...), custom_call_target="tpu_custom_call", output_to_operand_aliasing={{0}: (5, {}), {1}: (6, {}), {2}: (7, {}), {3}: (8, {})} | custom-call | flops 6442450944 | bytes 54591488 | tf_op jit(solution)/shard_map/pallas_call | solution.py:302
  126.7 0.1 add.22
  126.9 0.1 add.21
  127.0 0.3 add.20.refs_10_
  127.6 0.5 collective-permute-start.30
  128.0 0.1 collective-permute-start.29
  128.2 0.3 collective-permute-start.11
  128.5 22.8 %collective-permute-done.10.refs_6_ = bf16[3,1024,128]{2,1,0:T(8,128)(2,1)} collective-permute-done((bf16[3,1024,128]{2,1,0:T(8,128)(2,1)}, bf16[3,1024,128]{2,1,0:T(8,128)(2,1)}, u32[]{:S(2)}, u32[]{:S(2)}) %collective-permute-start.10) | collective-permute-done | bytes 786464 | tf_op jit(solution)/shard_map/ppermute | solution.py:333
  151.3 0.6 collective-permute-start.9
  151.8 15.2 %collective-permute-done.9.refs_5_ = bf16[3,1024,128]{2,1,0:T(8,128)(2,1)S(1)} collective-permute-done((bf16[3,1024,128]{2,1,0:T(8,128)(2,1)S(1)}, bf16[3,1024,128]{2,1,0:T(8,128)(2,1)S(1)}, u32[]{:S(2)}, u32[]{:S(2)}) %collective-permute-start.9) | collective-permute-done | bytes 786464 | tf_op jit(solution)/shard_map/ppermute | solution.py:333
  167.1 1.0 copy-done.7
  168.1 1.0 copy-done.8
  169.1 28.4 %shard_map.47 = (f32[4096,128]{1,0:T(8,128)}, f32[4096,128]{1,0:T(8,128)}) custom-call(s32[11]{0:T(128)} %stack.41.idx, bf16[1024,128]{1,0:T(8,128)(2,1)} %get-tuple-element.31.refs_0_, bf16[1024,128]{1,0:T(8,128)(2,1)} %copy-done.12, bf16[1024,128]{1,0:T(8,128)(2,1)} %copy-done.13, bf16[1024,128]{1,0:T(8,128)(2,1)} %collective-permute-done.5.refs_3_, ...), custom_call_target="tpu_custom_call" | custom-call | flops 8589934592 | bytes 44105728 | tf_op jit(solution)/shard_map/pallas_call | solution.py:302
  (83 shorter events, 0.5 us)
Async XLA Ops:
  0.6 43.0 %collective-permute-start.12 = (bf16[1024,512]{1,0:T(8,128)(2,1)}, bf16[1024,512]{1,0:T(8,128)(2,1)S(1)}, u32[]{:S(2)}, u32[]{:S(2)}) collective-permute-start(bf16[1024,512]{1,0:T(8,128)(2,1)} %refs_8_.1), channel_id=1, source_target_pairs={{0,8},{1,9},{2,10},{3,11},{4,12},{5,13},{6,14},{7,15},{8,0},{9,1},... | collective-permute-start | bytes 3145736 | tf_op jit(solution)/shard_map/ppermute | solution.py:333
  3.7 46.3 %collective-permute-start.13 = (bf16[1024,512]{1,0:T(8,128)(2,1)}, bf16[1024,512]{1,0:T(8,128)(2,1)S(1)}, u32[]{:S(2)}, u32[]{:S(2)}) collective-permute-start(bf16[1024,512]{1,0:T(8,128)(2,1)} %refs_8_.1), channel_id=1, source_target_pairs={{8,16},{9,17},{10,18},{11,19},{12,20},{13,21},{14,22},{15,23},{16,... | collective-permute-start | bytes 3145736 | tf_op jit(solution)/shard_map/ppermute | solution.py:333
  5.1 63.6 %copy-start.1 = (bf16[1024,512]{1,0:T(8,128)(2,1)S(1)}, bf16[1024,512]{1,0:T(8,128)(2,1)}, u32[]{:S(2)}) copy-start(bf16[1024,512]{1,0:T(8,128)(2,1)} %refs_8_.1) | copy-start | bytes 3145732
  8.4 11.1 %collective-permute-start.17 = (f32[8,512]{1,0:T(8,128)}, f32[8,512]{1,0:T(8,128)S(1)}, u32[]{:S(2)}, u32[]{:S(2)}) collective-permute-start(f32[8,512]{1,0:T(8,128)} %get-tuple-element.35.refs_4_), channel_id=1, source_target_pairs={{0,0},{1,8},{2,16},{3,24},{4,4},{5,12},{6,20},{7,28},{8,1},{9,9},{... | collective-permute-start | bytes 49160 | tf_op jit(solution)/shard_map/ppermute | solution.py:333
  9.8 22.8 %collective-permute-start.18 = (f32[8,512]{1,0:T(8,128)}, f32[8,512]{1,0:T(8,128)S(1)}, u32[]{:S(2)}, u32[]{:S(2)}) collective-permute-start(f32[8,512]{1,0:T(8,128)} %get-tuple-element.35.refs_4_), channel_id=1, source_target_pairs={{0,1},{1,9},{2,17},{3,25},{4,5},{5,13},{6,21},{7,29},{8,2},{9,10},... | collective-permute-start | bytes 49160 | tf_op jit(solution)/shard_map/ppermute | solution.py:333
  16.2 17.4 %collective-permute-start.19 = (f32[8,512]{1,0:T(8,128)}, f32[8,512]{1,0:T(8,128)S(1)}, u32[]{:S(2)}, u32[]{:S(2)}) collective-permute-start(f32[8,512]{1,0:T(8,128)} %get-tuple-element.35.refs_4_), channel_id=1, source_target_pairs={{0,2},{1,10},{2,18},{3,26},{4,6},{5,14},{6,22},{7,30},{8,3},{9,11}... | collective-permute-start | bytes 49160 | tf_op jit(solution)/shard_map/ppermute | solution.py:333
  19.5 31.9 %copy-start.21 = (f32[8,512]{1,0:T(8,128)}, f32[8,512]{1,0:T(8,128)S(1)}, u32[]{:S(2)}) copy-start(f32[8,512]{1,0:T(8,128)S(1)} %collective-permute-done.17.refs_0_) | copy-start | bytes 49156
  19.5 19.1 %collective-permute-start.20 = (f32[8,512]{1,0:T(8,128)}, f32[8,512]{1,0:T(8,128)S(1)}, u32[]{:S(2)}, u32[]{:S(2)}) collective-permute-start(f32[8,512]{1,0:T(8,128)} %get-tuple-element.35.refs_4_), channel_id=1, source_target_pairs={{0,3},{1,11},{2,19},{3,27},{4,7},{5,15},{6,23},{7,31},{8,0},{9,8},... | collective-permute-start | bytes 49160 | tf_op jit(solution)/shard_map/ppermute | solution.py:333
  32.6 18.8 %copy-start.22 = (f32[8,512]{1,0:T(8,128)}, f32[8,512]{1,0:T(8,128)S(1)}, u32[]{:S(2)}) copy-start(f32[8,512]{1,0:T(8,128)S(1)} %collective-permute-done.18.refs_1_) | copy-start | bytes 49156
  32.6 7.5 %collective-permute-start.21 = (f32[8,512]{1,0:T(8,128)}, f32[8,512]{1,0:T(8,128)S(1)}, u32[]{:S(2)}, u32[]{:S(2)}) collective-permute-start(f32[8,512]{1,0:T(8,128)} %get-tuple-element.35.refs_4_), channel_id=1, source_target_pairs={{0,8},{1,9},{2,10},{3,11},{4,12},{5,13},{6,14},{7,15},{8,16},{9,17... | collective-permute-start | bytes 49160 | tf_op jit(solution)/shard_map/ppermute | solution.py:333
  33.6 17.8 %copy-start.23 = (f32[8,512]{1,0:T(8,128)}, f32[8,512]{1,0:T(8,128)S(1)}, u32[]{:S(2)}) copy-start(f32[8,512]{1,0:T(8,128)S(1)} %collective-permute-done.19.refs_2_) | copy-start | bytes 49156
  33.6 9.9 %collective-permute-start.22 = (f32[8,512]{1,0:T(8,128)}, f32[8,512]{1,0:T(8,128)S(1)}, u32[]{:S(2)}, u32[]{:S(2)}) collective-permute-start(f32[8,512]{1,0:T(8,128)} %get-tuple-element.35.refs_4_), channel_id=1, source_target_pairs={{0,16},{1,17},{2,18},{3,19},{4,20},{5,21},{6,22},{7,23},{8,24},{9,... | collective-permute-start | bytes 49160 | tf_op jit(solution)/shard_map/ppermute | solution.py:333
  38.6 12.8 %copy-start.24 = (f32[8,512]{1,0:T(8,128)}, f32[8,512]{1,0:T(8,128)S(1)}, u32[]{:S(2)}) copy-start(f32[8,512]{1,0:T(8,128)S(1)} %collective-permute-done.20.refs_3_) | copy-start | bytes 49156
  38.6 6.6 %collective-permute-start.23 = (f32[8,512]{1,0:T(8,128)}, f32[8,512]{1,0:T(8,128)S(1)}, u32[]{:S(2)}, u32[]{:S(2)}) collective-permute-start(f32[8,512]{1,0:T(8,128)} %get-tuple-element.35.refs_4_), channel_id=1, source_target_pairs={{0,24},{1,25},{2,26},{3,27},{4,28},{5,29},{6,30},{7,31},{8,0},{9,1... | collective-permute-start | bytes 49160 | tf_op jit(solution)/shard_map/ppermute | solution.py:333
  40.1 11.3 %copy-start.25 = (f32[8,512]{1,0:T(8,128)}, f32[8,512]{1,0:T(8,128)S(1)}, u32[]{:S(2)}) copy-start(f32[8,512]{1,0:T(8,128)S(1)} %collective-permute-done.21.refs_5_) | copy-start | bytes 49156
  40.1 9.3 %collective-permute-start = (bf16[1024,128]{1,0:T(8,128)(2,1)}, bf16[1024,128]{1,0:T(8,128)(2,1)S(1)}, u32[]{:S(2)}, u32[]{:S(2)}) collective-permute-start(bf16[1024,128]{1,0:T(8,128)(2,1)} %get-tuple-element.28), channel_id=1, source_target_pairs={{0,1},{1,0},{2,3},{3,2},{4,5},{5,4},{6,7},{7,6},{8,9},{9,8},{10,11... | collective-permute-start | bytes 786440 | tf_op jit(solution)/shard_map/ppermute | solution.py:333
  43.5 7.9 %copy-start.26 = (f32[8,512]{1,0:T(8,128)}, f32[8,512]{1,0:T(8,128)S(1)}, u32[]{:S(2)}) copy-start(f32[8,512]{1,0:T(8,128)S(1)} %collective-permute-done.22.refs_6_) | copy-start | bytes 49156
  43.5 10.0 %collective-permute-start.1 = (bf16[1024,128]{1,0:T(8,128)(2,1)}, bf16[1024,128]{1,0:T(8,128)(2,1)S(1)}, u32[]{:S(2)}, u32[]{:S(2)}) collective-permute-start(bf16[1024,128]{1,0:T(8,128)(2,1)} %get-tuple-element.29), channel_id=1, source_target_pairs={{0,2},{1,3},{2,0},{3,1},{4,6},{5,7},{6,4},{7,5},{8,10},{9,11},{10,... | collective-permute-start | bytes 786440 | tf_op jit(solution)/shard_map/ppermute | solution.py:333
  43.7 83.8 %copy-start.2 = (bf16[1024,512]{1,0:T(8,128)(2,1)}, bf16[1024,512]{1,0:T(8,128)(2,1)S(1)}, u32[]{:S(2)}) copy-start(bf16[1024,512]{1,0:T(8,128)(2,1)S(1)} %collective-permute-done.12.refs_9_) | copy-start | bytes 3145732
  43.7 10.0 %collective-permute-start.2 = (bf16[1024,128]{1,0:T(8,128)(2,1)}, bf16[1024,128]{1,0:T(8,128)(2,1)S(1)}, u32[]{:S(2)}, u32[]{:S(2)}) collective-permute-start(bf16[1024,128]{1,0:T(8,128)(2,1)} %get-tuple-element.30), channel_id=1, source_target_pairs={{0,3},{1,2},{2,1},{3,0},{4,7},{5,6},{6,5},{7,4},{8,11},{9,10},{10,... | collective-permute-start | bytes 786440 | tf_op jit(solution)/shard_map/ppermute | solution.py:333
  45.2 41.9 %collective-permute-start.15 = (bf16[512,512]{1,0:T(8,128)(2,1)S(1)}, bf16[512,512]{1,0:T(8,128)(2,1)S(1)}, u32[]{:S(2)}, u32[]{:S(2)}) collective-permute-start(bf16[512,512]{1,0:T(8,128)(2,1)S(1)} %get-tuple-element.53), channel_id=1, source_target_pairs={{8,16},{9,17},{10,18},{11,19},{12,20},{13,21},{14,22},{15,23},{16,... | collective-permute-start | bytes 1572872 | tf_op jit(solution)/shard_map/ppermute | solution.py:333
  49.3 39.0 %collective-permute-start.25 = (bf16[512,512]{1,0:T(8,128)(2,1)S(1)}, bf16[512,512]{1,0:T(8,128)(2,1)S(1)}, u32[]{:S(2)}, u32[]{:S(2)}) collective-permute-start(bf16[512,512]{1,0:T(8,128)(2,1)S(1)} %get-tuple-element.52), channel_id=1, source_target_pairs={{8,16},{9,17},{10,18},{11,19},{12,20},{13,21},{14,22},{15,23},{16,... | collective-permute-start | bytes 1572872 | tf_op jit(solution)/shard_map/ppermute | solution.py:333
  50.0 59.2 %collective-permute-start.14 = (bf16[1024,512]{1,0:T(8,128)(2,1)S(1)}, bf16[1024,512]{1,0:T(8,128)(2,1)S(1)}, u32[]{:S(2)}, u32[]{:S(2)}) collective-permute-start(bf16[1024,512]{1,0:T(8,128)(2,1)S(1)} %collective-permute-done.13), channel_id=1, source_target_pairs={{8,0},{9,1},{10,2},{11,3},{12,4},{13,5},{14,6},{15,7},{16,24},{17,... | collective-permute-start | bytes 3145736 | tf_op jit(solution)/shard_map/ppermute | solution.py:333
  53.6 6.5 %collective-permute-start.24 = (f32[8,512]{1,0:T(8,128)}, f32[8,512]{1,0:T(8,128)S(1)}, u32[]{:S(2)}, u32[]{:S(2)}) collective-permute-start(f32[8,512]{1,0:T(8,128)} %get-tuple-element.37.own_stat.refs_21_), channel_id=1, source_target_pairs={{0,4},{1,5},{2,6},{3,7},{4,0},{5,1},{6,2},{7,3},{8,12},{9,13},{10,... | collective-permute-start | bytes 49160 | tf_op jit(solution)/shard_map/ppermute | solution.py:333
  57.4 11.3 %collective-permute-start.6 = (bf16[1024,128]{1,0:T(8,128)(2,1)}, bf16[1024,128]{1,0:T(8,128)(2,1)S(1)}, u32[]{:S(2)}, u32[]{:S(2)}) collective-permute-start(bf16[1024,128]{1,0:T(8,128)(2,1)} %get-tuple-element.32), channel_id=1, source_target_pairs={{0,8},{1,9},{2,10},{3,11},{4,12},{5,13},{6,14},{7,15},{8,16},{9,17... | collective-permute-start | bytes 786440 | tf_op jit(solution)/shard_map/ppermute | solution.py:333
  60.1 29.8 %copy-start.20 = (f32[8,512]{1,0:T(8,128)}, f32[8,512]{1,0:T(8,128)S(1)}, u32[]{:S(2)}) copy-start(f32[8,512]{1,0:T(8,128)S(1)} %collective-permute-done.24.mate_stat.refs_22_) | copy-start | bytes 49156
  60.1 24.7 %collective-permute-start.7 = (bf16[1024,128]{1,0:T(8,128)(2,1)}, bf16[1024,128]{1,0:T(8,128)(2,1)S(1)}, u32[]{:S(2)}, u32[]{:S(2)}) collective-permute-start(bf16[1024,128]{1,0:T(8,128)(2,1)} %get-tuple-element.33), channel_id=1, source_target_pairs={{0,16},{1,17},{2,18},{3,19},{4,20},{5,21},{6,22},{7,23},{8,24},{9,... | collective-permute-start | bytes 786440 | tf_op jit(solution)/shard_map/ppermute | solution.py:333
  68.7 33.6 %copy-start.17 = (bf16[1024,128]{1,0:T(8,128)(2,1)}, bf16[1024,128]{1,0:T(8,128)(2,1)S(1)}, u32[]{:S(2)}) copy-start(bf16[1024,128]{1,0:T(8,128)(2,1)S(1)} %collective-permute-done.6.refs_0_) | copy-start | bytes 786436
  68.7 59.5 %collective-permute-start.27 = (bf16[1024,512]{1,0:T(8,128)(2,1)S(1)}, bf16[1024,512]{1,0:T(8,128)(2,1)S(1)}, u32[]{:S(2)}, u32[]{:S(2)}) collective-permute-start(bf16[1024,512]{1,0:T(8,128)(2,1)S(1)} %copy-done.1), channel_id=1, source_target_pairs={{0,4},{1,5},{2,6},{3,7},{4,0},{5,1},{6,2},{7,3},{8,12},{9,13},{10,... | collective-permute-start | bytes 3145736 | tf_op jit(solution)/shard_map/ppermute | solution.py:333
  84.8 17.4 %collective-permute-start.8 = (bf16[1024,128]{1,0:T(8,128)(2,1)}, bf16[1024,128]{1,0:T(8,128)(2,1)S(1)}, u32[]{:S(2)}, u32[]{:S(2)}) collective-permute-start(bf16[1024,128]{1,0:T(8,128)(2,1)} %get-tuple-element.34), channel_id=1, source_target_pairs={{0,24},{1,25},{2,26},{3,27},{4,28},{5,29},{6,30},{7,31},{8,0},{9,1... | collective-permute-start | bytes 786440 | tf_op jit(solution)/shard_map/ppermute | solution.py:333
  87.1 22.1 %collective-permute-start.16 = (bf16[512,512]{1,0:T(8,128)(2,1)S(1)}, bf16[512,512]{1,0:T(8,128)(2,1)S(1)}, u32[]{:S(2)}, u32[]{:S(2)}) collective-permute-start(bf16[512,512]{1,0:T(8,128)(2,1)S(1)} %collective-permute-done.15), channel_id=1, source_target_pairs={{8,0},{9,1},{10,2},{11,3},{12,4},{13,5},{14,6},{15,7},{16,24},{17,... | collective-permute-start | bytes 1572872 | tf_op jit(solution)/shard_map/ppermute | solution.py:333
  88.4 24.4 %collective-permute-start.26 = (bf16[512,512]{1,0:T(8,128)(2,1)S(1)}, bf16[512,512]{1,0:T(8,128)(2,1)S(1)}, u32[]{:S(2)}, u32[]{:S(2)}) collective-permute-start(bf16[512,512]{1,0:T(8,128)(2,1)S(1)} %collective-permute-done.25), channel_id=1, source_target_pairs={{8,0},{9,1},{10,2},{11,3},{12,4},{13,5},{14,6},{15,7},{16,24},{17,... | collective-permute-start | bytes 1572872 | tf_op jit(solution)/shard_map/ppermute | solution.py:333
  89.9 13.1 %copy-start.11 = (bf16[1024,128]{1,0:T(8,128)(2,1)S(1)}, bf16[1024,128]{1,0:T(8,128)(2,1)}, u32[]{:S(2)}) copy-start(bf16[1024,128]{1,0:T(8,128)(2,1)} %get-tuple-element.31.refs_0_) | copy-start | bytes 786436
  103.0 24.5 %collective-permute-start.3 = (bf16[1024,128]{1,0:T(8,128)(2,1)S(1)}, bf16[1024,128]{1,0:T(8,128)(2,1)S(1)}, u32[]{:S(2)}, u32[]{:S(2)}) collective-permute-start(bf16[1024,128]{1,0:T(8,128)(2,1)S(1)} %copy-done.11), channel_id=1, source_target_pairs={{0,1},{1,0},{2,3},{3,2},{4,5},{5,4},{6,7},{7,6},{8,9},{9,8},{10,11... | collective-permute-start | bytes 786440 | tf_op jit(solution)/shard_map/ppermute | solution.py:333
  109.2 18.3 %collective-permute-start.4 = (bf16[1024,128]{1,0:T(8,128)(2,1)S(1)}, bf16[1024,128]{1,0:T(8,128)(2,1)S(1)}, u32[]{:S(2)}, u32[]{:S(2)}) collective-permute-start(bf16[1024,128]{1,0:T(8,128)(2,1)S(1)} %copy-done.11), channel_id=1, source_target_pairs={{0,2},{1,3},{2,0},{3,1},{4,6},{5,7},{6,4},{7,5},{8,10},{9,11},{10,... | collective-permute-start | bytes 786440 | tf_op jit(solution)/shard_map/ppermute | solution.py:333
  109.2 18.8 %collective-permute-start.5 = (bf16[1024,128]{1,0:T(8,128)(2,1)S(1)}, bf16[1024,128]{1,0:T(8,128)(2,1)}, u32[]{:S(2)}, u32[]{:S(2)}) collective-permute-start(bf16[1024,128]{1,0:T(8,128)(2,1)S(1)} %copy-done.11), channel_id=1, source_target_pairs={{0,3},{1,2},{2,1},{3,0},{4,7},{5,6},{6,5},{7,4},{8,11},{9,10},{10,... | collective-permute-start | bytes 786440 | tf_op jit(solution)/shard_map/ppermute | solution.py:333
  112.8 38.5 %collective-permute-start.10 = (bf16[3,1024,128]{2,1,0:T(8,128)(2,1)}, bf16[3,1024,128]{2,1,0:T(8,128)(2,1)}, u32[]{:S(2)}, u32[]{:S(2)}) collective-permute-start(bf16[3,1024,128]{2,1,0:T(8,128)(2,1)} %shard_map.43.refs_4_), channel_id=1, source_target_pairs={{0,2},{1,3},{2,0},{3,1},{4,6},{5,7},{6,4},{7,5},{8,10},{9,11},{10,... | collective-permute-start | bytes 2359304 | tf_op jit(solution)/shard_map/ppermute | solution.py:333
  127.3 41.8 %copy-start = (bf16[1024,512]{1,0:T(8,128)(2,1)}, bf16[1024,512]{1,0:T(8,128)(2,1)S(1)}, u32[]{:S(2)}) copy-start(bf16[1024,512]{1,0:T(8,128)(2,1)S(1)} %add.20.refs_10_) | copy-start | bytes 3145732
  127.4 41.7 %copy-start.3 = (bf16[1024,512]{1,0:T(8,128)(2,1)}, bf16[1024,512]{1,0:T(8,128)(2,1)S(1)}, u32[]{:S(2)}) copy-start(bf16[1024,512]{1,0:T(8,128)(2,1)S(1)} %pad_maximum_fusion.refs_11_) | copy-start | bytes 3145732
  127.4 41.6 %copy-start.12 = (bf16[1024,128]{1,0:T(8,128)(2,1)}, bf16[1024,128]{1,0:T(8,128)(2,1)S(1)}, u32[]{:S(2)}) copy-start(bf16[1024,128]{1,0:T(8,128)(2,1)S(1)} %collective-permute-done.3.refs_1_) | copy-start | bytes 786436
  127.5 39.6 %collective-permute-start.28 = (bf16[1024,512]{1,0:T(8,128)(2,1)S(1)}, bf16[1024,512]{1,0:T(8,128)(2,1)S(1)}, u32[]{:S(2)}, u32[]{:S(2)}) collective-permute-start(bf16[1024,512]{1,0:T(8,128)(2,1)S(1)} %collective-permute-done.12.refs_9_), channel_id=1, source_target_pairs={{0,4},{1,5},{2,6},{3,7},{4,0},{5,1},{6,2},{7,3},{8,12},{9,13},{10,... | collective-permute-start | bytes 3145736 | tf_op jit(solution)/shard_map/ppermute | solution.py:333
  127.5 41.5 %copy-start.13 = (bf16[1024,128]{1,0:T(8,128)(2,1)}, bf16[1024,128]{1,0:T(8,128)(2,1)S(1)}, u32[]{:S(2)}) copy-start(bf16[1024,128]{1,0:T(8,128)(2,1)S(1)} %collective-permute-done.4.refs_2_) | copy-start | bytes 786436
  127.6 39.5 %collective-permute-start.30 = (bf16[1024,512]{1,0:T(8,128)(2,1)S(1)}, bf16[1024,512]{1,0:T(8,128)(2,1)S(1)}, u32[]{:S(2)}, u32[]{:S(2)}) collective-permute-start(bf16[1024,512]{1,0:T(8,128)(2,1)S(1)} %pad_maximum_fusion.refs_11_), channel_id=1, source_target_pairs={{0,4},{1,5},{2,6},{3,7},{4,0},{5,1},{6,2},{7,3},{8,12},{9,13},{10,... | collective-permute-start | bytes 3145736 | tf_op jit(solution)/shard_map/ppermute | solution.py:333
  128.0 39.0 %collective-permute-start.29 = (bf16[1024,512]{1,0:T(8,128)(2,1)S(1)}, bf16[1024,512]{1,0:T(8,128)(2,1)S(1)}, u32[]{:S(2)}, u32[]{:S(2)}) collective-permute-start(bf16[1024,512]{1,0:T(8,128)(2,1)S(1)} %add.20.refs_10_), channel_id=1, source_target_pairs={{0,4},{1,5},{2,6},{3,7},{4,0},{5,1},{6,2},{7,3},{8,12},{9,13},{10,... | collective-permute-start | bytes 3145736 | tf_op jit(solution)/shard_map/ppermute | solution.py:333
  128.2 40.9 %copy-start.5 = (bf16[1024,512]{1,0:T(8,128)(2,1)}, bf16[1024,512]{1,0:T(8,128)(2,1)S(1)}, u32[]{:S(2)}) copy-start(bf16[1024,512]{1,0:T(8,128)(2,1)S(1)} %collective-permute-done.27.refs_12_) | copy-start | bytes 3145732
  128.2 23.7 %collective-permute-start.11 = (bf16[3,1024,128]{2,1,0:T(8,128)(2,1)S(1)}, bf16[3,1024,128]{2,1,0:T(8,128)(2,1)S(1)}, u32[]{:S(2)}, u32[]{:S(2)}) collective-permute-start(bf16[3,1024,128]{2,1,0:T(8,128)(2,1)S(1)} %copy-done.4), channel_id=1, source_target_pairs={{0,3},{1,2},{2,1},{3,0},{4,7},{5,6},{6,5},{7,4},{8,11},{9,10},{10,... | collective-permute-start | bytes 2359304 | tf_op jit(solution)/shard_map/ppermute | solution.py:333
  151.3 15.8 %collective-permute-start.9 = (bf16[3,1024,128]{2,1,0:T(8,128)(2,1)S(1)}, bf16[3,1024,128]{2,1,0:T(8,128)(2,1)S(1)}, u32[]{:S(2)}, u32[]{:S(2)}) collective-permute-start(bf16[3,1024,128]{2,1,0:T(8,128)(2,1)S(1)} %copy-done.4), channel_id=1, source_target_pairs={{0,1},{1,0},{2,3},{3,2},{4,5},{5,4},{6,7},{7,6},{8,9},{9,8},{10,11... | collective-permute-start | bytes 2359304 | tf_op jit(solution)/shard_map/ppermute | solution.py:333
  151.8 17.3 %copy-start.9 = (bf16[3,1024,128]{2,1,0:T(8,128)(2,1)}, bf16[3,1024,128]{2,1,0:T(8,128)(2,1)S(1)}, u32[]{:S(2)}) copy-start(bf16[3,1024,128]{2,1,0:T(8,128)(2,1)S(1)} %collective-permute-done.11.refs_7_) | copy-start | bytes 2359300
  (11 other events, 25.0 us)
